TPU v7x, 32 devices: a whole 2x2x4 slice. The times are simulated.
32 devices in a mesh: dp: 8 (over y, x, core), seq: 4 (over z).
Axes of the slice: x: 2, y: 2, z: 4, core: 2. Of those that a mesh axis runs over, the one named last changes fastest.
Arguments:
- tokens: bfloat16 [2, 8, 1024, 1024], P(None, 'dp', 'seq'), may hold values from -6 to 6
- segments: int32 [2, 8, 1024], P(None, 'dp'), may hold values from 0 to 3, never falling along the last dimension, each value on 1 to 800 neighbouring positions
- ln1_gain: float32 [1024], P(('dp', 'seq')), may hold values from 0.1 to 1.9
- in_weight: float32 [1024, 3072], P(('dp', 'seq')), may hold values from -0.1875 to 0.1875
- conv_kernel: float32 [3, 1024], P(None, ('dp', 'seq')), may hold values from -3 to 3
- out_weight: float32 [1024, 1024], P(('dp', 'seq')), may hold values from -0.1875 to 0.1875
- ln2_gain: float32 [1024], P(('dp', 'seq')), may hold values from 0.1 to 1.9
- gate_weight: float32 [1024, 4608], P(('dp', 'seq')), may hold values from -0.1875 to 0.1875
- up_weight: float32 [1024, 4608], P(('dp', 'seq')), may hold values from -0.1875 to 0.1875
- down_weight: float32 [4608, 1024], P(('dp', 'seq')), may hold values from -0.09375 to 0.09375
- cotangent: bfloat16 [2, 8, 1024, 1024], P(None, 'dp', 'seq'), may hold values from -6 to 6
Outputs:
- output: bfloat16 [2, 8, 1024, 1024], P(None, 'dp', 'seq')
- grad_tokens: bfloat16 [2, 8, 1024, 1024], P(None, 'dp', 'seq')
- grad_ln1: float32 [1024], P(('dp', 'seq'))
- grad_in: float32 [1024, 3072], P(('dp', 'seq'))
- grad_kernel: float32 [3, 1024], P(None, ('dp', 'seq'))
- grad_out: float32 [1024, 1024], P(('dp', 'seq'))
- grad_ln2: float32 [1024], P(('dp', 'seq'))
- grad_gate: float32 [1024, 4608], P(('dp', 'seq'))
- grad_up: float32 [1024, 4608], P(('dp', 'seq'))
- grad_down: float32 [4608, 1024], P(('dp', 'seq'))
Inputs may be any that keep to these rules, and one draw needn't show every extreme that they name: `segments`: along each sequence the document numbers start at 0 and never fall; equal numbers mark one document.
All inputs are finite; a program needn't handle non-finite values.
Results may differ from a plain program's by a relative error of at most 0.012.
The roundings to bfloat16 on the way count: a program that leaves them out, or rounds other values in their place, can miss the bound.
Values may be sent and summed in bfloat16 or wider, within the bound.
A program may use at most 192 MiB of HBM per device.

v0:
```python
import jax
import jax.numpy as jnp
from jax import lax
from jax.sharding import PartitionSpec as P

eps = 1e-05


def shifted(block, axis, distance):
    devices = range(lax.axis_size(axis))
    route = [(i - distance, i) for i in devices if i - distance in devices]
    return lax.ppermute(block, axis, route)


def matmul(left, right):
    return jnp.dot(left, right, preferred_element_type=jnp.float32)


def norm_parts(values):
    inverse = lax.rsqrt(jnp.mean(values * values, axis=-1, keepdims=True) + eps)
    return (inverse, values * inverse)


def norm_back(grad_hidden, normed, inverse, gain):
    grad_normed = grad_hidden * gain
    inner_mean = jnp.mean(grad_normed * normed, axis=-1, keepdims=True)
    return inverse * (grad_normed - normed * inner_mean)


def per_device(
    tokens,
    segments,
    ln1_gain,
    in_weight,
    conv_kernel,
    out_weight,
    ln2_gain,
    gate_weight,
    up_weight,
    down_weight,
    cotangent,
):
    micro_count = tokens.shape[0]
    row_count = tokens.shape[2]
    width = tokens.shape[3]
    taps = conv_kernel.shape[0]
    offset = lax.axis_index("seq") * row_count
    low_gain1 = ln1_gain.astype(jnp.bfloat16)
    low_in = in_weight.astype(jnp.bfloat16)
    low_kernel = conv_kernel.astype(jnp.bfloat16)
    low_out = out_weight.astype(jnp.bfloat16)
    low_gain2 = ln2_gain.astype(jnp.bfloat16)
    low_gate = gate_weight.astype(jnp.bfloat16)
    low_up = up_weight.astype(jnp.bfloat16)
    low_down = down_weight.astype(jnp.bfloat16)
    shard_totals = None
    full_totals = None
    out_list = []
    grad_list = []
    for micro_index in range(micro_count):
        weights = (
            lax.all_gather(low_gain1, ("dp", "seq"), axis=0, tiled=True),
            lax.all_gather(low_in, ("dp", "seq"), axis=0, tiled=True),
            lax.all_gather(low_kernel, ("dp", "seq"), axis=1, tiled=True),
            lax.all_gather(low_out, ("dp", "seq"), axis=0, tiled=True),
            lax.all_gather(low_gain2, ("dp", "seq"), axis=0, tiled=True),
            lax.all_gather(low_gate, ("dp", "seq"), axis=0, tiled=True),
            lax.all_gather(low_up, ("dp", "seq"), axis=0, tiled=True),
            lax.all_gather(low_down, ("dp", "seq"), axis=0, tiled=True),
        )
        gain_one = weights[0].astype(jnp.float32)
        kernel = weights[2].astype(jnp.float32)
        gain_two = weights[4].astype(jnp.float32)
        seg_line = segments[micro_index, 0]
        fill = jnp.full((2,), -1, jnp.int32)
        seg_pad = jnp.concatenate([fill, seg_line, fill])
        window = lax.dynamic_slice_in_dim(seg_pad, offset, row_count + 4)
        masks = [
            (window[tap : tap + row_count + 2] == window[2 : row_count + 4]).astype(jnp.float32)
            for tap in range(taps)
        ]
        tokens_f = tokens[micro_index, 0].astype(jnp.float32)
        inverse_one, normed_one = norm_parts(tokens_f)
        hidden_one = (normed_one * gain_one).astype(jnp.bfloat16)
        projected = matmul(hidden_one, weights[1])
        b_part = projected[:, :width]
        c_part = projected[:, width : 2 * width]
        x_part = projected[:, 2 * width :]
        mixed = (b_part * x_part).astype(jnp.bfloat16)
        prev_rows = shifted(mixed[row_count - 2 :], "seq", 1)
        extended = jnp.concatenate([prev_rows, mixed], axis=0).astype(jnp.float32)
        conv_out = jnp.zeros((row_count, width), jnp.float32)
        for tap in range(taps):
            conv_out = (
                conv_out
                + kernel[tap] * extended[tap : tap + row_count] * masks[tap][:row_count, None]
            )
        gated = (c_part * conv_out).astype(jnp.bfloat16)
        resid = tokens_f + matmul(gated, weights[3])
        inverse_two, normed_two = norm_parts(resid)
        hidden_two = (normed_two * gain_two).astype(jnp.bfloat16)
        gate_pre = matmul(hidden_two, weights[5])
        up_pre = matmul(hidden_two, weights[6])
        sigmoid_gate = jax.nn.sigmoid(gate_pre)
        activated = gate_pre * sigmoid_gate
        inner = (activated * up_pre).astype(jnp.bfloat16)
        ffn_out = matmul(inner, weights[7])
        out_list.append((resid + ffn_out).astype(jnp.bfloat16))
        back_weights = (
            lax.all_gather(low_gain1, ("dp", "seq"), axis=0, tiled=True),
            lax.all_gather(low_in, ("dp", "seq"), axis=0, tiled=True),
            lax.all_gather(low_kernel, ("dp", "seq"), axis=1, tiled=True),
            lax.all_gather(low_out, ("dp", "seq"), axis=0, tiled=True),
            lax.all_gather(low_gain2, ("dp", "seq"), axis=0, tiled=True),
            lax.all_gather(low_gate, ("dp", "seq"), axis=0, tiled=True),
            lax.all_gather(low_up, ("dp", "seq"), axis=0, tiled=True),
            lax.all_gather(low_down, ("dp", "seq"), axis=0, tiled=True),
        )
        grad_final = cotangent[micro_index, 0]
        grad_inner = matmul(grad_final, back_weights[7].T)
        part_down = matmul(inner.T, grad_final)
        grad_gate_pre = (
            grad_inner * up_pre * sigmoid_gate * (1.0 + gate_pre * (1.0 - sigmoid_gate))
        ).astype(jnp.bfloat16)
        grad_up_pre = (grad_inner * activated).astype(jnp.bfloat16)
        grad_hidden_two = matmul(grad_gate_pre, back_weights[5].T) + matmul(
            grad_up_pre, back_weights[6].T
        )
        part_gate = matmul(hidden_two.T, grad_gate_pre)
        part_up = matmul(hidden_two.T, grad_up_pre)
        part_gain2 = jnp.sum(grad_hidden_two * normed_two, axis=0)
        grad_resid = grad_final.astype(jnp.float32) + norm_back(
            grad_hidden_two, normed_two, inverse_two, gain_two
        )
        grad_branch = grad_resid.astype(jnp.bfloat16)
        grad_gated = matmul(grad_branch, back_weights[3].T)
        part_out = matmul(gated.T, grad_branch)
        grad_c = grad_gated * conv_out
        grad_conv = (grad_gated * c_part).astype(jnp.bfloat16)
        next_rows = shifted(grad_conv[:2], "seq", -1)
        grad_extended = jnp.concatenate([grad_conv, next_rows], axis=0).astype(jnp.float32)
        grad_mixed = jnp.zeros((row_count, width), jnp.float32)
        kernel_terms = []
        for tap in range(taps):
            weighted = grad_extended * masks[tap][:, None]
            grad_mixed = grad_mixed + kernel[tap] * weighted[2 - tap : 2 - tap + row_count]
            kernel_terms.append(
                jnp.sum(weighted[:row_count] * extended[tap : tap + row_count], axis=0)
            )
        part_kernel = jnp.stack(kernel_terms, axis=0)
        grad_proj = jnp.concatenate(
            [grad_mixed * x_part, grad_c, grad_mixed * b_part], axis=1
        ).astype(jnp.bfloat16)
        grad_hidden_one = matmul(grad_proj, back_weights[1].T)
        part_in = matmul(hidden_one.T, grad_proj)
        part_gain1 = jnp.sum(grad_hidden_one * normed_one, axis=0)
        grad_input = grad_resid + norm_back(grad_hidden_one, normed_one, inverse_one, gain_one)
        grad_list.append(grad_input.astype(jnp.bfloat16))
        parts = (
            part_gain1,
            part_in,
            part_kernel,
            part_out,
            part_gain2,
            part_gate,
            part_up,
            part_down,
        )
        full_totals = (
            parts
            if full_totals is None
            else tuple((first + second for first, second in zip(full_totals, parts)))
        )
    shard_totals = (
        lax.psum_scatter(full_totals[0], ("dp", "seq"), scatter_dimension=0, tiled=True),
        lax.psum_scatter(full_totals[1], ("dp", "seq"), scatter_dimension=0, tiled=True),
        lax.psum_scatter(full_totals[2], ("dp", "seq"), scatter_dimension=1, tiled=True),
        lax.psum_scatter(full_totals[3], ("dp", "seq"), scatter_dimension=0, tiled=True),
        lax.psum_scatter(full_totals[4], ("dp", "seq"), scatter_dimension=0, tiled=True),
        lax.psum_scatter(full_totals[5], ("dp", "seq"), scatter_dimension=0, tiled=True),
        lax.psum_scatter(full_totals[6], ("dp", "seq"), scatter_dimension=0, tiled=True),
        lax.psum_scatter(full_totals[7], ("dp", "seq"), scatter_dimension=0, tiled=True),
    )
    output = jnp.stack(out_list, axis=0)[:, None]
    grad_tokens = jnp.stack(grad_list, axis=0)[:, None]
    return (
        output,
        grad_tokens,
        shard_totals[0],
        shard_totals[1],
        shard_totals[2],
        shard_totals[3],
        shard_totals[4],
        shard_totals[5],
        shard_totals[6],
        shard_totals[7],
    )


def solution(mesh):
    in_specs = (
        P(None, "dp", "seq", None),
        P(None, "dp", None),
        P(("dp", "seq")),
        P(("dp", "seq"), None),
        P(None, ("dp", "seq")),
        P(("dp", "seq"), None),
        P(("dp", "seq")),
        P(("dp", "seq"), None),
        P(("dp", "seq"), None),
        P(("dp", "seq"), None),
        P(None, "dp", "seq", None),
    )
    out_specs = (
        P(None, "dp", "seq", None),
        P(None, "dp", "seq", None),
        P(("dp", "seq")),
        P(("dp", "seq"), None),
        P(None, ("dp", "seq")),
        P(("dp", "seq"), None),
        P(("dp", "seq")),
        P(("dp", "seq"), None),
        P(("dp", "seq"), None),
        P(("dp", "seq"), None),
    )
    return jax.shard_map(
        per_device, mesh=mesh, in_specs=in_specs, out_specs=out_specs, check_vma=False
    )
```

profile of v0, /device:TPU:0, one launch (start us, length us, event | category | flops | bytes accessed | tf_op | source)
XLA Modules:
  0.0 1562.4 jit_solution(12153144668011816908)
XLA Ops:
  10.8 1.8 convert_element_type.171
  12.7 1.8 convert_element_type.172
  15.9 42.2 %all-reduce.5 = (bf16[1024]{0:T(1024)(128)(2,1)S(1)}, bf16[1024]{0:T(1024)(128)(2,1)S(1)}) all-reduce(bf16[1024]{0:T(1024)(128)(2,1)S(1)} %dynamic-update-slice, bf16[1024]{0:T(1024)(128)(2,1)S(1)} %dynamic-update-slice.1), channel_id=1, replica_groups=mesh['dp'=8,'seq'=4] {'dp','seq'}, use_global_device_ids=true, to_apply=%add | all-reduce | flops 2048 | bytes 8192
  58.1 66.1 %all-gather = bf16[32,32,3]{1,2,0:T(4,128)(2,1)S(1)} all-gather(bf16[1,32,3]{1,2,0:T(4,128)(2,1)S(1)} %convert_bitcast_fusion), channel_id=1, replica_groups=mesh['dp'=8,'seq'=4] {'dp','seq'}, dimensions={0}, use_global_device_ids=true | all-gather | bytes 6336 | tf_op jit(solution)/shard_map/all_gather | solution.py:64
  125.3 5.1 fusion.65
  132.1 1.9 fusion.62
  134.2 1.9 collective-permute-start.1
  137.6 2.5 multiply_convert_fusion.18
  140.1 2.4 all-gather.9.cloned.1.call-done
  142.6 2.7 multiply_reduce_fusion.7
  147.3 79.6 %all-gather.11.cloned.1.call-done = bf16[1024,4608]{1,0:T(8,128)(2,1)} async-done(((bf16[32,4608]{1,0:T(8,128)(2,1)}), bf16[1024,4608]{1,0:T(8,128)(2,1)}) %all-gather.11.cloned.1.call-update) | async-done | bytes 9437200 | tf_op jit(solution)/shard_map/all_gather | solution.py:67
  226.9 8.4 fusion.79
  235.3 74.9 %all-gather.13.cloned.1.call-done = bf16[1024,4608]{1,0:T(8,128)(2,1)} async-done(((bf16[32,4608]{1,0:T(8,128)(2,1)}), bf16[1024,4608]{1,0:T(8,128)(2,1)}) %all-gather.13.cloned.1.call-update) | async-done | bytes 9437200 | tf_op jit(solution)/shard_map/all_gather | solution.py:68
  310.2 7.9 fusion.80
  318.1 75.4 %all-gather.15.cloned.1.call-done = bf16[4608,1024]{1,0:T(8,128)(2,1)} async-done(((bf16[144,1024]{1,0:T(8,128)(2,1)}), bf16[4608,1024]{1,0:T(8,128)(2,1)}) %all-gather.15.cloned.1.call-update) | async-done | bytes 9437200 | tf_op jit(solution)/shard_map/all_gather | solution.py:69
  393.5 9.9 multiply_convert_fusion.2
  403.5 6.9 fusion.83
  410.5 8.5 multiply_reduce_fusion.1
  419.0 2.6 fusion.81
  421.6 8.0 fusion.82
  429.7 13.7 multiply_convert_fusion
  443.4 4.4 fusion.84
  447.9 5.6 multiply_reduce_fusion
  458.7 1.8 multiply_convert_fusion.7
  461.8 2.8 fusion.57
  466.3 1.9 fusion.31
  468.2 2.6 collective-permute-done.2
  471.1 1.9 fusion.33
  474.3 5.2 convolution_add_fusion.4
  484.0 1.9 fusion.39
  486.0 6.4 convolution_add_fusion.3
  493.4 9.7 fusion.85
  503.2 12.1 convolution_add_fusion.2
  515.4 9.8 fusion.86
  525.2 12.2 convolution_add_fusion.1
  538.6 9.7 fusion.46
  548.3 12.2 convolution_add_fusion
  561.7 7.1 fusion.12
  568.9 6.4 fusion.13
  576.5 2.0 fusion.38
  578.6 3.0 fusion.20
  581.6 40.0 %all-reduce.4 = (f32[1024]{0:T(1024)S(1)}, f32[1024]{0:T(1024)S(1)}) all-reduce(f32[1024]{0:T(1024)S(1)} %add.169, f32[1024]{0:T(1024)S(1)} %add.173), channel_id=2, replica_groups=mesh['dp'=8,'seq'=4] {'dp','seq'}, use_global_device_ids=true, to_apply=%region_10.0.clone | all-reduce | flops 2048 | bytes 16384
  622.8 2.1 fusion.42
  627.3 128.4 %reduce-scatter.11.cloned.1.call-done = f32[32,1024]{1,0:T(8,128)} async-done(((f32[1024,1024]{1,0:T(8,128)}), f32[32,1024]{1,0:T(8,128)}) %reduce-scatter.11.cloned.1.call-update) | async-done | bytes 131088 | tf_op jit(solution)/shard_map/reduce_scatter | solution.py:178
  755.7 161.8 %reduce-scatter.9.cloned.1.call-done = f32[32,3072]{1,0:T(8,128)} async-done(((f32[1024,3072]{1,0:T(8,128)}), f32[32,3072]{1,0:T(8,128)}) %reduce-scatter.9.cloned.1.call-update) | async-done | bytes 393232 | tf_op jit(solution)/shard_map/reduce_scatter | solution.py:176
  917.6 212.8 %reduce-scatter.13.cloned.1.call-done = f32[32,4608]{1,0:T(8,128)} async-done(((f32[1024,4608]{1,0:T(8,128)}), f32[32,4608]{1,0:T(8,128)}) %reduce-scatter.13.cloned.1.call-update) | async-done | bytes 589840 | tf_op jit(solution)/shard_map/reduce_scatter | solution.py:180
  1130.3 212.5 %reduce-scatter.15.cloned.1.call-done = f32[32,4608]{1,0:T(8,128)} async-done(((f32[1024,4608]{1,0:T(8,128)}), f32[32,4608]{1,0:T(8,128)}) %reduce-scatter.15.cloned.1.call-update) | async-done | bytes 589840 | tf_op jit(solution)/shard_map/reduce_scatter | solution.py:181
  1342.8 212.6 %reduce-scatter.17.cloned.1.call-done = f32[144,1024]{1,0:T(8,128)} async-done(((f32[4608,1024]{1,0:T(8,128)}), f32[144,1024]{1,0:T(8,128)}) %reduce-scatter.17.cloned.1.call-update) | async-done | bytes 589840 | tf_op jit(solution)/shard_map/reduce_scatter | solution.py:182
  (222 shorter events, 33.6 us)
Async XLA Ops:
  7.2 7.4 copy-start.51
  7.2 8.2 copy-start.56
  7.2 8.2 copy-start.57
  7.2 50.9 %copy-start.54 = (f32[3,32]{1,0:T(4,128)S(1)}, f32[3,32]{1,0:T(4,128)}, u32[]{:S(2)}) copy-start(f32[3,32]{1,0:T(4,128)} %param.15) | copy-start | bytes 1156
  7.2 117.2 %copy-start.52 = (s32[2,1,1024]{2,1,0:T(1,128)S(1)}, s32[2,1,1024]{2,1,0:T(1,128)}, u32[]{:S(2)}) copy-start(s32[2,1,1024]{2,1,0:T(1,128)} %param.12) | copy-start | bytes 24580
  7.2 117.7 %copy-start.10 = (bf16[2,1,256,1024]{3,2,1,0:T(8,128)(2,1)S(1)}, bf16[2,1,256,1024]{3,2,1,0:T(8,128)(2,1)}, u32[]{:S(2)}) copy-start(bf16[2,1,256,1024]{3,2,1,0:T(8,128)(2,1)} %param.11) | copy-start | bytes 3145732
  7.2 118.0 %all-gather.7.cloned.1.call-start = ((), (), s32[]{:S(2)}) async-start(), calls=%async_computation.6 | async-start | bytes 6488064 | tf_op jit(solution)/shard_map/all_gather | solution.py:63
  9.1 133.4 %all-gather.9.cloned.1.call-start = ((), (), s32[]{:S(2)}) async-start(), calls=%async_computation.7 | async-start | bytes 2162688 | tf_op jit(solution)/shard_map/all_gather | solution.py:65
  10.7 216.1 %all-gather.11.cloned.1.call-start = ((), (), s32[]{:S(2)}) async-start(), calls=%async_computation.8 | async-start | bytes 9732096 | tf_op jit(solution)/shard_map/all_gather | solution.py:67
  12.6 297.6 %all-gather.13.cloned.1.call-start = ((), (), s32[]{:S(2)}) async-start(), calls=%async_computation.9 | async-start | bytes 9732096 | tf_op jit(solution)/shard_map/all_gather | solution.py:68
  14.5 379.0 %all-gather.15.cloned.1.call-start = ((), (), s32[]{:S(2)}) async-start(), calls=%async_computation.10 | async-start | bytes 9732096 | tf_op jit(solution)/shard_map/all_gather | solution.py:69
  15.3 610.6 %reduce-scatter.19.cloned.1.call-start = ((), (), s32[]{:S(2)}) async-start(), calls=%async_computation.16 | async-start | bytes 540672
  125.2 6.9 copy-start.55
  130.4 7.3 copy-start.6
  130.5 5.6 collective-permute-start
  134.2 3.2 collective-permute-start.1
  147.2 162.9 %copy-start.2 = (bf16[256,1024]{1,0:T(8,128)(2,1)}, bf16[256,1024]{1,0:T(8,128)(2,1)S(1)}, u32[]{:S(2)}) copy-start(bf16[256,1024]{1,0:T(8,128)(2,1)S(1)} %multiply_convert_fusion.17) | copy-start | bytes 1572868
  403.4 7.0 copy-start.27
  403.4 7.0 copy-start.26
  403.4 7.0 copy-start.21
  403.4 7.0 copy-start.46
  403.5 15.5 slice-start
  403.5 15.5 slice-start.1
  410.4 8.5 slice-start.2
  421.6 8.1 copy-start.15
  447.8 5.7 copy-start.16
  447.8 5.7 copy-start.22
  447.9 5.7 copy-start.50
  454.1 7.7 copy-start
  460.5 5.5 collective-permute-start.3
  464.6 6.1 collective-permute-start.2
  474.1 281.7 %reduce-scatter.11.cloned.1.call-start = ((), (), s32[]{:S(2)}) async-start(), calls=%async_computation.12 | async-start | bytes 4325376 | tf_op jit(solution)/shard_map/reduce_scatter | solution.py:178
  479.5 438.0 %reduce-scatter.9.cloned.1.call-start = ((), (), s32[]{:S(2)}) async-start(), calls=%async_computation.11 | async-start | bytes 12976128 | tf_op jit(solution)/shard_map/reduce_scatter | solution.py:176
  492.4 10.8 copy-start.5
  492.4 637.9 %reduce-scatter.13.cloned.1.call-start = ((), (), s32[]{:S(2)}) async-start(), calls=%async_computation.13 | async-start | bytes 19464192 | tf_op jit(solution)/shard_map/reduce_scatter | solution.py:180
  493.4 9.8 copy-start.30
  515.3 827.5 %reduce-scatter.15.cloned.1.call-start = ((), (), s32[]{:S(2)}) async-start(), calls=%async_computation.14 | async-start | bytes 19464192 | tf_op jit(solution)/shard_map/reduce_scatter | solution.py:181
  515.4 9.8 copy-start.29
  537.4 1018.1 %reduce-scatter.17.cloned.1.call-start = ((), (), s32[]{:S(2)}) async-start(), calls=%async_computation.15 | async-start | bytes 19464192 | tf_op jit(solution)/shard_map/reduce_scatter | solution.py:182
  538.6 9.7 copy-start.14
  561.7 7.1 copy-start.23
  561.7 7.2 copy-start.31
  561.7 14.7 slice-start.3
  568.9 7.6 copy-start.33
  568.9 7.5 copy-start.35
  568.9 7.5 copy-start.37
  568.9 7.5 slice-start.4
  578.6 44.2 %copy-start.1 = (f32[256,1024]{1,0:T(8,128)S(1)}, f32[256,1024]{1,0:T(8,128)}, u32[]{:S(2)}) copy-start(f32[256,1024]{1,0:T(8,128)} %copy-done) | copy-start | bytes 3145732
  (30 other events, 77.0 us)
Sparse Core Ops, SparseCore 0:
  11.5 72.4 all-gather.6
  87.5 54.9 all-gather.8
  145.9 80.8 all-gather.10
  229.5 80.6 all-gather.12
  312.8 80.6 all-gather.14
  474.2 133.9 reduce-scatter.18
  611.1 144.6 reduce-scatter.10
  763.4 154.1 reduce-scatter.8
  924.5 205.7 reduce-scatter.12
  1137.2 205.6 reduce-scatter.14
  1349.8 205.6 reduce-scatter.16
where the time goes:
time: 1570 us; the launch traced here: 1560 us
  waiting for transfers between devices  1160 us (74%)
  matrix products  190 us (12%)
  blocking collectives  148 us (9%)
  other arithmetic  25.4 us (2%)
    reduce_scatter x1, waiting for transfers between devices, per_device(): lax.psum_scatter(full_totals[5], ('dp', 'seq'), scatter_dimension=0, tile...  213 us
    reduce_scatter x1, waiting for transfers between devices, per_device(): lax.psum_scatter(full_totals[7], ('dp', 'seq'), scatter_dimension=0, tile...  213 us
    reduce_scatter x1, waiting for transfers between devices, per_device(): lax.psum_scatter(full_totals[6], ('dp', 'seq'), scatter_dimension=0, tile...  212 us
    dot_general x30, matrix products, matmul(): return jnp.dot(left, right, preferred_element_type=jnp.float32)  190 us
    reduce_scatter x1, waiting for transfers between devices, per_device(): lax.psum_scatter(full_totals[1], ('dp', 'seq'), scatter_dimension=0, tile...  162 us
    reduce_scatter x1, waiting for transfers between devices, per_device(): lax.psum_scatter(full_totals[3], ('dp', 'seq'), scatter_dimension=0, tile...  128 us
    unnamed x2, blocking collectives  82.2 us
    all_gather x1, waiting for transfers between devices, per_device(): lax.all_gather(low_gate, ('dp', 'seq'), axis=0, tiled=True)  79.6 us
  transfers between devices with their start and end apart: 15, of which 12 were waited for; matrix products, arithmetic and copies ran while one was open for 10% of the time, Pallas kernels for 0%

commit v1 on v0

--- a/solution.py
+++ b/solution.py
@@ -1,9 +1,498 @@
+import functools
 import jax
 import jax.numpy as jnp
 from jax import lax
+from jax.experimental import pallas as pl
+from jax.experimental.pallas import tpu as pltpu
 from jax.sharding import PartitionSpec as P
 
+BF = jnp.bfloat16
+F32 = jnp.float32
 eps = 1e-05
+MESH = pl.DeviceIdType.MESH
+NN = (((1,), (0,)), ((), ()))
+NT = (((1,), (1,)), ((), ()))
+TN = (((0,), (0,)), ((), ()))
+TP = 4
+
+
+def mm(left, right, dims):
+    return lax.dot_general(left, right, dims, preferred_element_type=F32)
+
+
+def when(pred, body):
+    if pred is True:
+        body()
+    else:
+        pl.when(pred)(body)
+
+
+class Place:
+    def __init__(self, nz):
+        dp = lax.axis_index("dp")
+        self.y = dp // TP
+        self.i = dp % TP
+        self.z = lax.axis_index("seq")
+        self.nz = nz
+        self.x = self.i // 2
+        self.c = self.i % 2
+
+    def member(self, t):
+        x = 1 - self.x if t // 2 else self.x
+        c = 1 - self.c if t % 2 else self.c
+        return x * 2 + c
+
+    def at(self, y=None, i=None, z=None):
+        y = self.y if y is None else y
+        i = self.i if i is None else i
+        z = self.z if z is None else z
+        return (y * TP + i, z)
+
+
+class Copies:
+    def __init__(self):
+        self.pending = []
+
+    def send(self, src, dst, ssem, rsem, device, pred=True):
+        def make():
+            return pltpu.make_async_remote_copy(
+                src_ref=src, dst_ref=dst, send_sem=ssem, recv_sem=rsem,
+                device_id=device, device_id_type=MESH)
+        when(pred, lambda: make().start())
+        self.pending.append((pred, make))
+
+    def local(self, src, dst, sem):
+        pltpu.make_async_copy(src, dst, sem).start()
+
+    def arrived(self, ref, ssem, rsem, device, pred=True):
+        when(pred, lambda: pltpu.make_async_remote_copy(
+            src_ref=ref, dst_ref=ref, send_sem=ssem, recv_sem=rsem,
+            device_id=device, device_id_type=MESH).wait_recv())
+
+    def drain(self, count=None):
+        done = self.pending[:count]
+        self.pending = self.pending[len(done):]
+        for pred, make in done:
+            when(pred, lambda make=make: make().wait_send())
+
+
+def entry_barrier(p):
+    bar = pltpu.get_barrier_semaphore()
+    for t in range(1, TP):
+        pl.semaphore_signal(bar, inc=1, device_id=p.at(i=p.member(t)), device_id_type=MESH)
+    pl.semaphore_signal(bar, inc=1, device_id=p.at(y=1 - p.y), device_id_type=MESH)
+    for step, pred in ((-1, p.z > 0), (1, p.z < p.nz - 1)):
+        pl.when(pred)(lambda step=step: pl.semaphore_signal(
+            bar, inc=1, device_id=p.at(z=p.z + step), device_id_type=MESH))
+    count = TP + (p.z > 0).astype(jnp.int32) + (p.z < p.nz - 1).astype(jnp.int32)
+    pl.semaphore_wait(bar, count)
+
+
+def ffn_body(parts, nz, h_in, df_in, gus, ds, f_out, dh_out, ogu_out, od_out,
+             H, dF, WGU, WD, dHa, Zb, dAb, dGb, GGU, GD, RY, ZGU, OGU, ZD, YD, FD, FIN,
+             LX, SX, sem_h, sem_l, s_p0, r_p0, s_z, r_z, s_y, r_y,
+             s_dz, r_dz, s_dy, r_dy, s_gy, r_gy, s_gz, r_gz, s_gt, r_gt,
+             s_ez, r_ez, s_ey, r_ey, s_x, r_x):
+    p = Place(nz)
+    z = p.z
+    rows = h_in.shape[0]
+    width = h_in.shape[1]
+    shard = gus.shape[2]
+    npos = 2 * nz
+    offs = [sum(parts[:k]) for k in range(len(parts))]
+    CH = [(offs[k] * npos, parts[k] * npos) for k in range(len(parts))]
+    K = len(parts)
+    cp = Copies()
+    first, last = z == 0, z == nz - 1
+    inner_l, inner_r = z > 0, z < nz - 1
+
+    def cols(k):
+        return slice(CH[k][0], CH[k][0] + CH[k][1])
+
+    def rws(k):
+        return slice(offs[k], offs[k] + parts[k])
+
+    cx = Copies()
+    cp.local(h_in, H.at[0], sem_l.at[0])
+    cp.local(df_in, dF.at[0], sem_l.at[1])
+    cp.local(gus.at[p.i], WGU.at[p.y, p.i, z], sem_l.at[2])
+    for k in range(K):
+        cp.local(ds.at[rws(k)], WD[k].at[p.y, z], sem_l.at[3 + k])
+    entry_barrier(p)
+
+    def p0(k):
+        for t in (2, 3, 1):
+            m = p.member(t)
+            cp.send(gus.at[m, :, :, cols(k)], WGU.at[p.y, p.i, z, :, :, cols(k)],
+                    s_p0.at[k, t - 1], r_p0.at[k, t - 1], p.at(i=m))
+
+    def acts(src, dst, q):
+        pltpu.make_async_copy(src, dst.at[0], sem_l.at[q]).wait()
+        for t in (2, 1):
+            cp.send(dst.at[0], dst.at[t], sem_h.at[q, 0, t - 1], sem_h.at[q, 1, t - 1], p.at(i=p.member(t)))
+
+    def acts_wait(dst, q, t):
+        cp.arrived(dst.at[t], sem_h.at[q, 0, t - 1], sem_h.at[q, 1, t - 1], p.at(i=p.member(t)))
+
+    def acts_forward(dst, q):
+        acts_wait(dst, q, 2)
+        cp.send(dst.at[2], dst.at[3], sem_h.at[q, 0, 2], sem_h.at[q, 1, 2], p.at(i=p.member(1)))
+
+    def gu_blk(k, y, zz):
+        return WGU.at[y, :, zz, :, :, cols(k)]
+
+    def gu_zsend(k, zz, right):
+        pred = inner_r if right else inner_l
+        d = 1 if right else 0
+        b = gu_blk(k, p.y, zz)
+        cp.send(b, b, s_z.at[k, d, zz], r_z.at[k, zz], p.at(z=z + 1 if right else z - 1), pred)
+
+    def gu_ysend(k, zz, pred=True):
+        b = gu_blk(k, p.y, zz)
+        cp.send(b, b, s_y.at[k, zz], r_y.at[k, zz], p.at(y=1 - p.y), pred)
+
+    def flow_ag_gu(k):
+        for t in (1, 2, 3):
+            m = p.member(t)
+            cp.arrived(WGU.at[p.y, m, z, :, :, cols(k)], s_p0.at[k, t - 1], r_p0.at[k, t - 1], p.at(i=m))
+        gu_zsend(k, z, True)
+        gu_zsend(k, z, False)
+        gu_ysend(k, z)
+        for s in range(1, nz):
+            for right in (True, False):
+                yield
+                zz = z - s if right else z + s
+                got = zz >= 0 if right else zz <= nz - 1
+                more = got & (inner_r if right else inner_l)
+
+                def arrive(zz=zz):
+                    cp2 = gu_blk(k, p.y, zz)
+                    cp.arrived(cp2, s_z.at[k, 0, zz], r_z.at[k, zz], p.at())
+                pl.when(got)(arrive)
+                b = gu_blk(k, p.y, zz)
+                d = 1 if right else 0
+                cp.send(b, b, s_z.at[k, d, zz], r_z.at[k, zz], p.at(z=z + 1 if right else z - 1), more)
+                gu_ysend(k, zz, got)
+        for zz in range(nz):
+            yield
+            cp.arrived(gu_blk(k, 1 - p.y, zz), s_y.at[k, zz], r_y.at[k, zz], p.at(y=1 - p.y))
+
+    def flow_ag_d(k):
+        W = WD[k]
+        own = W.at[p.y, z]
+        cp.send(own, own, s_dy.at[k], r_dy.at[k], p.at(y=1 - p.y))
+
+        def zs(y, yi, zz, right, pred):
+            b = W.at[y, zz]
+            d = 1 if right else 0
+            cp.send(b, b, s_dz.at[k, yi, d, zz], r_dz.at[k, yi, zz], p.at(z=z + 1 if right else z - 1), pred)
+        zs(p.y, p.y, z, True, inner_r)
+        zs(p.y, p.y, z, False, inner_l)
+        yield
+        cp.arrived(W.at[1 - p.y, z], s_dy.at[k], r_dy.at[k], p.at(y=1 - p.y))
+        zs(1 - p.y, 1 - p.y, z, True, inner_r)
+        zs(1 - p.y, 1 - p.y, z, False, inner_l)
+        for s in range(1, nz):
+            for right in (True, False):
+                yield
+                zz = z - s if right else z + s
+                got = zz >= 0 if right else zz <= nz - 1
+                more = got & (inner_r if right else inner_l)
+                for y in (p.y, 1 - p.y):
+                    pl.when(got)(lambda y=y, zz=zz: cp.arrived(
+                        W.at[y, zz], s_dz.at[k, y, 0, zz], r_dz.at[k, y, zz], p.at()))
+                    zs(y, y, zz, right, more)
+
+    order = [nz - 1, 0] + list(range(1, nz - 1))[::-1]
+
+    def flow_rs_gu(k):
+        c = cols(k)
+        for zz in order:
+            cp.send(GGU.at[1 - p.y, :, zz, :, :, c], RY.at[:, zz, :, :, c],
+                    s_gy.at[k, zz], r_gy.at[k, zz], p.at(y=1 - p.y))
+
+        def ry_wait(zz):
+            cp.arrived(RY.at[:, zz, :, :, c], s_gy.at[k, zz], r_gy.at[k, zz], p.at(y=1 - p.y))
+
+        def zwait(sl):
+            cp.arrived(ZGU.at[sl, :, :, :, c], s_gz.at[k, 0, 0], r_gz.at[k, sl], p.at())
+        for zz in order:
+            yield
+            right, left = z < zz, z > zz
+            ry_wait(zz)
+            both = (right & inner_l) | (left & inner_r)
+
+            def add3(zz=zz):
+                zwait(zz)
+                for j in range(TP):
+                    GGU[p.y, j, zz, :, :, c] = (
+                        GGU[p.y, j, zz, :, :, c].astype(F32) + RY[j, zz, :, :, c].astype(F32)
+                        + ZGU[zz, j, :, :, c].astype(F32)).astype(BF)
+
+            def add2(zz=zz):
+                for j in range(TP):
+                    GGU[p.y, j, zz, :, :, c] = (
+                        GGU[p.y, j, zz, :, :, c].astype(F32) + RY[j, zz, :, :, c].astype(F32)).astype(BF)
+            pl.when(both)(add3)
+            pl.when(jnp.logical_and(z != zz, jnp.logical_not(both)))(add2)
+            src = GGU.at[p.y, :, zz, :, :, c]
+            sl_r = zz
+            cp.send(src, ZGU.at[sl_r, :, :, :, c], s_gz.at[k, 1, zz], r_gz.at[k, sl_r], p.at(z=z + 1), right)
+            sl_l = jnp.where(z - 1 == zz, nz, zz)
+            cp.send(src, ZGU.at[sl_l, :, :, :, c], s_gz.at[k, 0, zz], r_gz.at[k, sl_l], p.at(z=z - 1), left)
+        yield
+        pl.when(inner_l)(lambda: zwait(z))
+        pl.when(inner_r)(lambda: zwait(nz))
+        for j in range(TP):
+            FIN[j, :, :, c] = (
+                GGU[p.y, j, z, :, :, c].astype(F32) + RY[j, z, :, :, c].astype(F32)
+                + ZGU[z, j, :, :, c].astype(F32) + ZGU[nz, j, :, :, c].astype(F32)).astype(BF)
+        for t in (2, 3, 1):
+            m = p.member(t)
+            cp.send(FIN.at[m, :, :, c], OGU.at[p.i, :, :, c], s_gt.at[k, t - 1], r_gt.at[k, t - 1], p.at(i=m))
+        OGU[p.i, :, :, c] = FIN[p.i, :, :, c]
+        yield
+        for t in (1, 2, 3):
+            m = p.member(t)
+            cp.arrived(OGU.at[m, :, :, c], s_gt.at[k, t - 1], r_gt.at[k, t - 1], p.at(i=m))
+
+    def flow_rs_d(k):
+        G, L = GD[k], ZD[k]
+
+        def zwait(sl):
+            cp.arrived(L.at[sl], s_ez.at[k, 0, 0], r_ez.at[k, sl], p.at())
+        for zz in order:
+            yield
+            right, left = z < zz, z > zz
+            both = (right & inner_l) | (left & inner_r)
+
+            def add2(zz=zz):
+                zwait(zz)
+                for y in range(2):
+                    G[y, zz] = (G[y, zz].astype(F32) + L[zz, y].astype(F32)).astype(BF)
+            pl.when(both)(add2)
+            src = G.at[:, zz]
+            cp.send(src, L.at[zz], s_ez.at[k, 1, zz], r_ez.at[k, zz], p.at(z=z + 1), right)
+            sl_l = jnp.where(z - 1 == zz, nz, zz)
+            cp.send(src, L.at[sl_l], s_ez.at[k, 0, zz], r_ez.at[k, sl_l], p.at(z=z - 1), left)
+        yield
+        pl.when(inner_l)(lambda: zwait(z))
+        pl.when(inner_r)(lambda: zwait(nz))
+        for y in range(2):
+            FD[k][y] = (G[y, z].astype(F32) + L[z, y].astype(F32) + L[nz, y].astype(F32)).astype(BF)
+        cp.send(FD[k].at[1 - p.y], YD[k], s_ey.at[k], r_ey.at[k], p.at(y=1 - p.y))
+        yield
+        cp.arrived(YD[k], s_ey.at[k], r_ey.at[k], p.at(y=1 - p.y))
+        od_out[rws(k), :] = FD[k][p.y].astype(F32) + YD[k][...].astype(F32)
+
+    def zero_left():
+        ZGU[0] = jnp.zeros(ZGU.shape[1:], BF)
+        for k in range(K):
+            ZD[k][0] = jnp.zeros(ZD[k].shape[1:], BF)
+
+    def zero_right():
+        ZGU[nz] = jnp.zeros(ZGU.shape[1:], BF)
+        for k in range(K):
+            ZD[k][nz] = jnp.zeros(ZD[k].shape[1:], BF)
+
+    for k in range(K):
+        p0(k)
+    acts(h_in, H, 0)
+    acts(df_in, dF, 1)
+    pl.when(first)(zero_left)
+    pl.when(last)(zero_right)
+    pltpu.make_async_copy(gus.at[p.i], WGU.at[p.y, p.i, z], sem_l.at[2]).wait()
+    for k in range(K):
+        pltpu.make_async_copy(ds.at[rws(k)], WD[k].at[p.y, z], sem_l.at[3 + k]).wait()
+
+    flows = []
+
+    def pump(n=1):
+        for _ in range(n):
+            for f in list(flows):
+                if next(f, "end") == "end":
+                    flows.remove(f)
+
+    def run(gen):
+        for _ in gen:
+            pass
+        if gen in flows:
+            flows.remove(gen)
+
+    ag = [(flow_ag_gu(k), flow_ag_d(k)) for k in range(K)]
+    live = []
+    for k in range(K):
+        for g in ag[k]:
+            next(g)
+            flows.append(g)
+        if k < K - 1:
+            pump(2)
+    acts_forward(H, 0)
+    acts_forward(dF, 1)
+
+    def fwd_mid(k, t):
+        c0, cn = CH[k]
+        c = cols(k)
+        wg = WGU[:, :, :, 0, :, c].reshape(width, cn)
+        wu = WGU[:, :, :, 1, :, c].reshape(width, cn)
+        wd = WD[k][...].reshape(cn, width)
+        a = mm(H[t], wg, NN)
+        g = mm(H[t], wu, NN)
+        dz = mm(dF[t], wd, NT)
+        sg = 1.0 / (1.0 + jnp.exp(-a))
+        act = a * sg
+        Zb[t, :, c] = (act * g).astype(BF)
+        dAb[t, :, :cn] = (dz * g * sg * (1.0 + a * (1.0 - sg))).astype(BF)
+        dGb[t, :, :cn] = (dz * act).astype(BF)
+        d = mm(dAb[t, :, :cn], wg, NT) + mm(dGb[t, :, :cn], wu, NT)
+        if k == 0:
+            dHa[t] = d
+        else:
+            dHa[t] += d
+
+    def ffn_out(t):
+        f = None
+        for k in range(K):
+            v = mm(Zb[t, :, cols(k)], WD[k][...].reshape(CH[k][1], width), NN)
+            f = v if f is None else f + v
+        return f
+
+    def grads(k):
+        c0, cn = CH[k]
+        c = cols(k)
+        tok = TP * rows
+        for w, src in ((0, dAb), (1, dGb)):
+            def body(m, _, w=w, src=src):
+                y, j = m // 2, (m % 2) * 2
+                f = 2 * nz * shard
+                ms = pl.ds(pl.multiple_of(m * f, f), f)
+                v = mm(H[:, :, ms].reshape(tok, f), src[:, :, :cn].reshape(tok, cn), TN)
+                GGU[y, pl.ds(j, 2), :, w, :, c] = v.astype(BF).reshape(2, nz, shard, cn)
+                return 0
+            lax.fori_loop(0, TP, body, 0)
+        r = parts[k]
+        for b in range(cn // 128):
+            v = mm(Zb[:, :, c0 + b * 128:c0 + (b + 1) * 128].reshape(tok, 128), dF[...].reshape(tok, width), TN).astype(BF)
+            lo = b * 128
+            while lo < (b + 1) * 128:
+                pos, q = lo // r, lo % r
+                n = min(r - q, (b + 1) * 128 - lo)
+                GD[k][pos // nz, pos % nz, q:q + n] = v[lo - b * 128:lo - b * 128 + n]
+                lo += n
+
+    def x_send1(q, e, value):
+        SX[e] = value.astype(BF)
+        cx.send(SX.at[e], LX.at[q, e], s_x.at[q, e], r_x.at[q, e], p.at(i=p.member(1)))
+
+    def x_wait(q, e):
+        cx.arrived(LX.at[q, e], s_x.at[q, e], r_x.at[q, e], p.at(i=p.member(2 if e == 2 else 1)))
+
+    def x_send2(q, acc):
+        x_wait(q, 1)
+        SX[2] = (acc[...] + LX[q, 1].astype(F32)).astype(BF)
+        cx.send(SX.at[2], LX.at[q, 2], s_x.at[q, 2], r_x.at[q, 2], p.at(i=p.member(2)))
+
+    def x_final(q, acc, out):
+        x_wait(q, 0)
+        x_wait(q, 2)
+        acc[...] += LX[q, 0].astype(F32) + LX[q, 2].astype(F32)
+        pltpu.make_async_copy(acc, out, sem_l.at[q]).start()
+
+    for k in range(K):
+        for g in ag[k]:
+            run(g)
+        if k == 0:
+            for t in (1, 3):
+                for q, dst in ((0, H), (1, dF)):
+                    acts_wait(dst, q, t)
+
+        def tbody(n, _, k=k):
+            fwd_mid(k, n)
+            return 0
+        lax.fori_loop(0, TP, tbody, 0)
+        pump(2)
+        if k == K - 1:
+            x_send1(0, 0, dHa[1])
+            x_send1(0, 1, dHa[3])
+        grads(k)
+        for g in (flow_rs_d(k), flow_rs_gu(k)):
+            next(g)
+            flows.append(g)
+        pump(1)
+    x_send2(0, dHa.at[2])
+    pump(1)
+    cx.drain(2)
+    x_send1(1, 0, ffn_out(1))
+    x_send1(1, 1, ffn_out(3))
+    pump(1)
+    dHa[1] = ffn_out(2)
+    dHa[3] = ffn_out(0)
+    pump(1)
+    x_final(0, dHa.at[0], dh_out)
+    cx.drain(1)
+    x_send2(1, dHa.at[1])
+    while flows:
+        pump(1)
+    x_final(1, dHa.at[3], f_out)
+    ogu_out[...] = OGU[...]
+    pltpu.make_async_copy(dHa.at[0], dh_out, sem_l.at[0]).wait()
+    pltpu.make_async_copy(dHa.at[3], f_out, sem_l.at[1]).wait()
+    cp.drain()
+    cx.drain()
+
+
+def ffn_call(h, df, gus, ds, parts, nz, cid):
+    rows, width = h.shape
+    shard, cols = gus.shape[2], gus.shape[3]
+    K = len(parts)
+    dr = ds.shape[0]
+    V = pl.BlockSpec(memory_space=pltpu.VMEM)
+    A = pl.BlockSpec(memory_space=pl.ANY)
+    D = pltpu.SemaphoreType.DMA
+    maxc = max(parts) * 2 * nz
+    scratch = [
+        pltpu.VMEM((TP, rows, width), BF),
+        pltpu.VMEM((TP, rows, width), BF),
+        pltpu.VMEM((2, TP, nz, 2, shard, cols), BF),
+        [pltpu.VMEM((2, nz, r, width), BF) for r in parts],
+        pltpu.VMEM((TP, rows, width), F32),
+        pltpu.VMEM((TP, rows, cols), BF),
+        pltpu.VMEM((TP, rows, maxc), BF),
+        pltpu.VMEM((TP, rows, maxc), BF),
+        pltpu.VMEM((2, TP, nz, 2, shard, cols), BF),
+        [pltpu.VMEM((2, nz, r, width), BF) for r in parts],
+        pltpu.VMEM((TP, nz, 2, shard, cols), BF),
+        pltpu.VMEM((nz + 1, TP, 2, shard, cols), BF),
+        pltpu.VMEM((TP, 2, shard, cols), BF),
+        [pltpu.VMEM((nz + 1, 2, r, width), BF) for r in parts],
+        [pltpu.VMEM((r, width), BF) for r in parts],
+        [pltpu.VMEM((2, r, width), BF) for r in parts],
+        pltpu.VMEM((TP, 2, shard, cols), BF),
+        pltpu.VMEM((2, 3, rows, width), BF),
+        pltpu.VMEM((3, rows, width), BF),
+        D((2, 2, 3)), D((3 + K,)),
+        D((K, 3)), D((K, 3)),
+        D((K, 2, nz)), D((K, nz)), D((K, nz)), D((K, nz)),
+        D((K, 2, 2, nz)), D((K, 2, nz)), D((K,)), D((K,)),
+        D((K, nz)), D((K, nz)), D((K, 2, nz)), D((K, nz + 1)), D((K, 3)), D((K, 3)),
+        D((K, 2, nz)), D((K, nz + 1)), D((K,)), D((K,)),
+        D((2, 3)), D((2, 3)),
+    ]
+    return pl.pallas_call(
+        functools.partial(ffn_body, parts, nz),
+        name="ffn",
+        out_shape=(
+            jax.ShapeDtypeStruct((rows, width), F32),
+            jax.ShapeDtypeStruct((rows, width), F32),
+            jax.ShapeDtypeStruct((TP, 2, shard, cols), BF),
+            jax.ShapeDtypeStruct((dr, width), F32),
+        ),
+        in_specs=[A, A, V, V],
+        out_specs=[A, A, V, V],
+        scratch_shapes=scratch,
+        compiler_params=pltpu.CompilerParams(
+            collective_id=cid, has_side_effects=True, vmem_limit_bytes=66_900_000),
+    )(h, df, gus, ds)
 
 
 def shifted(block, axis, distance):
@@ -27,7 +516,7 @@
     return inverse * (grad_normed - normed * inner_mean)
 
 
-def per_device(
+def plain_device(
     tokens,
     segments,
     ln1_gain,
@@ -197,6 +686,129 @@
     )
 
 
+def cut_columns(w, parts, ny, nz):
+    rows, shard = w.shape[0], w.shape[1] // (ny * TP * nz)
+    cut = w.astype(BF).reshape(rows, ny, TP, nz, shard)
+    pieces, start = [], 0
+    for size in parts:
+        piece = cut[..., start : start + size].transpose(2, 0, 1, 3, 4)
+        pieces.append(piece.reshape(TP, rows, ny * nz * size))
+        start += size
+    return jnp.concatenate(pieces, axis=-1)
+
+
+def join_columns(g, parts, ny, nz):
+    rows = g.shape[1]
+    pieces, start, npos = [], 0, ny * nz
+    for size in parts:
+        piece = g[:, :, npos * start : npos * (start + size)].reshape(TP, rows, ny, nz, size)
+        pieces.append(piece.transpose(1, 2, 0, 3, 4))
+        start += size
+    return jnp.concatenate(pieces, axis=-1).reshape(rows, -1).astype(F32)
+
+
+def fast_device(
+    parts,
+    tokens,
+    segments,
+    ln1_gain,
+    in_weight,
+    conv_kernel,
+    out_weight,
+    ln2_gain,
+    gate_weight,
+    up_weight,
+    down_weight,
+    cotangent,
+):
+    micro, _, count, width = tokens.shape
+    taps = conv_kernel.shape[0]
+    nz = lax.axis_size("seq")
+    ny = lax.axis_size("dp") // TP
+    rows = micro * count
+    both = ("dp", "seq")
+    x = tokens.reshape(rows, width).astype(F32)
+    w_in = lax.all_gather(in_weight.astype(BF), both, axis=0, tiled=True)
+    w_out = lax.all_gather(out_weight.astype(BF), both, axis=0, tiled=True)
+    small = jnp.concatenate([ln1_gain[None], ln2_gain[None], conv_kernel], axis=0).astype(BF)
+    small = lax.all_gather(small, both, axis=1, tiled=True).astype(F32)
+    gain_one, gain_two, kernel = small[0], small[1], small[2:]
+
+    offset = lax.axis_index("seq") * count
+    fill = jnp.full((micro, 2), -1, jnp.int32)
+    seg_pad = jnp.concatenate([fill, segments[:, 0], fill], axis=1)
+    window = lax.dynamic_slice_in_dim(seg_pad, offset, count + 4, axis=1)
+    masks = [
+        (window[:, tap : tap + count + 2] == window[:, 2 : count + 4]).astype(F32)[..., None]
+        for tap in range(taps)
+    ]
+    inv1, norm1 = norm_parts(x)
+    h1 = (norm1 * gain_one).astype(BF)
+    proj = matmul(h1, w_in)
+    b, c, u = (proj[:, k * width : (k + 1) * width] for k in range(3))
+    mixed = (b * u).astype(BF).reshape(micro, count, width)
+    prev = shifted(mixed[:, count - 2 :], "seq", 1)
+    ext = jnp.concatenate([prev, mixed], axis=1).astype(F32)
+    conv = sum(kernel[t] * ext[:, t : t + count] * masks[t][:, :count] for t in range(taps))
+    conv = conv.reshape(rows, width)
+    gated = (c * conv).astype(BF)
+    resid = x + matmul(gated, w_out)
+    inv2, norm2 = norm_parts(resid)
+    h2 = (norm2 * gain_two).astype(BF)
+
+    df = cotangent.reshape(rows, width)
+    gus = jnp.stack([cut_columns(gate_weight, parts, ny, nz), cut_columns(up_weight, parts, ny, nz)], axis=1)
+    f, dh2, gu, gd = ffn_call(h2, df, gus, down_weight.astype(BF), parts, nz, 0)
+    output = (resid + f).astype(BF)
+    g_gate = join_columns(gu[:, 0], parts, ny, nz)
+    g_up = join_columns(gu[:, 1], parts, ny, nz)
+
+    g_gain2 = jnp.sum(dh2 * norm2, axis=0)
+    dr = df.astype(F32) + norm_back(dh2, norm2, inv2, gain_two)
+    do = dr.astype(BF)
+    dy = matmul(do, w_out.T)
+    g_out = matmul(gated.T, do)
+    dc = dy * conv
+    dconv = (dy * c).astype(BF).reshape(micro, count, width)
+    after = shifted(dconv[:, :2], "seq", -1)
+    gext = jnp.concatenate([dconv, after], axis=1).astype(F32)
+    dmix = jnp.zeros((micro, count, width), F32)
+    kterms = []
+    for t in range(taps):
+        weighted = gext * masks[t]
+        dmix = dmix + kernel[t] * weighted[:, 2 - t : 2 - t + count]
+        kterms.append(jnp.sum(weighted[:, :count] * ext[:, t : t + count], axis=(0, 1)))
+    dmix = dmix.reshape(rows, width)
+    dproj = jnp.concatenate([dmix * u, dc, dmix * b], axis=1).astype(BF)
+    dh1 = matmul(dproj, w_in.T)
+    g_in = matmul(h1.T, dproj)
+    g_gain1 = jnp.sum(dh1 * norm1, axis=0)
+    gx = (dr + norm_back(dh1, norm1, inv1, gain_one)).astype(BF)
+    g_small = jnp.stack([g_gain1, g_gain2] + kterms, axis=0)
+    g_small = lax.psum_scatter(g_small, both, scatter_dimension=1, tiled=True)
+    g_in = lax.psum_scatter(g_in, both, scatter_dimension=0, tiled=True)
+    g_out = lax.psum_scatter(g_out, both, scatter_dimension=0, tiled=True)
+    shape = tokens.shape
+    return (
+        output.reshape(shape), gx.reshape(shape), g_small[0], g_in, g_small[2:], g_out,
+        g_small[1], g_gate, g_up, gd,
+    )
+
+
+def row_parts(mesh, down_shape):
+    nd, nz = mesh.shape["dp"], mesh.shape["seq"]
+    if nd != 2 * TP:
+        return None
+    per = down_shape[0] // (nd * nz)
+    if per % 16:
+        return None
+    sizes, left = [], per
+    while left:
+        sizes.append(min(64, left))
+        left -= sizes[-1]
+    return tuple(sizes)
+
+
 def solution(mesh):
     in_specs = (
         P(None, "dp", "seq", None),
@@ -223,6 +835,12 @@
         P(("dp", "seq"), None),
         P(("dp", "seq"), None),
     )
-    return jax.shard_map(
-        per_device, mesh=mesh, in_specs=in_specs, out_specs=out_specs, check_vma=False
-    )
+
+    def run(*arrays):
+        parts = row_parts(mesh, arrays[9].shape)
+        device = plain_device if parts is None else functools.partial(fast_device, parts)
+        return jax.shard_map(
+            device, mesh=mesh, in_specs=in_specs, out_specs=out_specs, check_vma=False
+        )(*arrays)
+
+    return run

time: 1570 us -> 901 us (0.57)
  waiting for transfers between devices: 1160 us -> 458 us
  Pallas kernels: 0 us -> 245 us
  matrix products: 190 us -> 29.8 us
  blocking collectives: 148 us -> 71.1 us
  local copies, waits for them, and re-layouts: 12.2 us -> 43.3 us
    reduce_scatter x5 -> x2, waiting for transfers between devices: 928 us -> 306 us  [the longest x1 162 us: fast_device(): g_in = lax.psum_scatter(g_in, both, scatter_dimension=0, tiled=True)]
    pallas_call x0 -> x1, Pallas kernels: none -> 245 us  [ffn_call(): pl.pallas_call(functools.partial(ffn_body, parts, nz), name='ffn', out_sh...]
    all_gather x5 -> x2, waiting for transfers between devices: 232 us -> 39.5 us  [the longest x1 39.5 us: fast_device(): w_out = lax.all_gather(out_weight.astype(BF), both, axis=0, tiled=True)]
    dot_general x30 -> x6, matrix products: 190 us -> 29.8 us  [matmul(): return jnp.dot(left, right, preferred_element_type=jnp.float32)]
    unnamed x12 -> x6, waiting for transfers between devices: 0.18 us -> 89.6 us
    unnamed x2 -> x0, blocking collectives: 82.2 us -> none
    ppermute x4 -> x2, waiting for transfers between devices: 3.78 us -> 23.2 us  [shifted(): return lax.ppermute(block, axis, route)]
  transfers between devices with their start and end apart: 15 -> 7, of which waited for: 12 -> 6; matrix products, arithmetic and copies ran while one was open for 10% -> 8% of each run, Pallas kernels for 0% -> 0%
where the time goes in v1:
time: 901 us; the launch traced here: 893 us
  waiting for transfers between devices  458 us (51%)
  Pallas kernels  245 us (27%)
  blocking collectives  71.1 us (8%)
  local copies, waits for them, and re-layouts  43.3 us (5%)
  matrix products  29.8 us (3%)
  other arithmetic  27.3 us (3%)
  between operations  14.9 us (2%)
    pallas_call x1, Pallas kernels, ffn_call(): pl.pallas_call(functools.partial(ffn_body, parts, nz), name='ffn', out_sh...  245 us
    reduce_scatter x1, waiting for transfers between devices, fast_device(): g_in = lax.psum_scatter(g_in, both, scatter_dimension=0, tiled=True)  162 us
    reduce_scatter x1, waiting for transfers between devices, fast_device(): g_out = lax.psum_scatter(g_out, both, scatter_dimension=0, tiled=True)  144 us
    unnamed x6, waiting for transfers between devices  89.6 us
    all_gather x1, blocking collectives, fast_device(): small = lax.all_gather(small, both, axis=1, tiled=True).astype(F32)  71.1 us
    all_gather x1, waiting for transfers between devices, fast_device(): w_out = lax.all_gather(out_weight.astype(BF), both, axis=0, tiled=True)  39.5 us
    dot_general x6, matrix products, matmul(): return jnp.dot(left, right, preferred_element_type=jnp.float32)  29.8 us
    ppermute x2, waiting for transfers between devices, shifted(): return lax.ppermute(block, axis, route)  23.2 us
  transfers between devices with their start and end apart: 7, of which 6 were waited for; matrix products, arithmetic and copies ran while one was open for 8% of the time, Pallas kernels for 0%

profile of v1, /device:TPU:0, one launch (start us, length us, event | category | flops | bytes accessed | tf_op | source)
XLA Modules:
  0.0 893.0 jit_solution(3138970595337307970)
XLA Ops:
  7.3 1.7 convert_element_type.88
  9.1 1.5 convert_element_type.94
  11.4 1.5 fusion.19
  12.9 71.1 %all-gather = bf16[32,32,5]{1,2,0:T(8,128)(2,1)S(1)} all-gather(bf16[1,32,5]{1,2,0:T(8,128)(2,1)S(1)} %maximum_bitcast_fusion.2), channel_id=1, replica_groups=mesh['dp'=8,'seq'=4] {'dp','seq'}, dimensions={0}, use_global_device_ids=true | all-gather | bytes 10560 | tf_op jit(solution)/shard_map/all_gather | solution.py:734
  86.6 0.9 reshape.139
  89.2 0.9 pad_maximum_fusion.3.gus
  90.4 5.9 fusion.34
  96.7 1.4 collective-permute-start
  98.1 1.0 convert_element_type.98.ds
  101.1 1.4 copy-done.3
  102.9 39.5 %all-gather.6.cloned.1.call-done = bf16[1024,1024]{1,0:T(8,128)(2,1)} async-done(((bf16[32,1024]{1,0:T(8,128)(2,1)}), bf16[1024,1024]{1,0:T(8,128)(2,1)}) %all-gather.6.cloned.1.call-update) | async-done | bytes 2097168 | tf_op jit(solution)/shard_map/all_gather | solution.py:732
  142.4 2.9 multiply_reduce_fusion.3
  145.4 1.4 copy-done.5
  146.8 1.2 multiply_convert_fusion.1.h_in
  148.0 245.2 %ffn.1 = (f32[512,1024]{1,0:T(8,128)}, f32[512,1024]{1,0:T(8,128)}, bf16[4,2,32,1152]{3,2,1,0:T(8,128)(2,1)}, f32[144,1024]{1,0:T(8,128)}) custom-call(bf16[512,1024]{1,0:T(8,128)(2,1)} %multiply_convert_fusion.1.h_in, bf16[512,1024]{1,0:T(8,128)(2,1)} %bitcast.139, bf16[4,2,32,1152]{3,2,1,0:T(8,128)(2,1)} %pad_maximum_fusion.3.gus, ...), custom_call_target="tpu_custom_call" | custom-call | tf_op jit(solution)/shard_map/ffn/pallas_call | solution.py:481
  393.2 3.0 multiply_reduce_fusion.1
  396.2 4.9 multiply_add_fusion
  401.3 1.3 fusion.7
  402.6 1.3 collective-permute-start.1
  403.9 22.9 %collective-permute-done.1 = bf16[2,2,1024]{2,1,0:T(2,128)(2,1)S(1)} collective-permute-done((bf16[2,2,1024]{2,1,0:T(2,128)(2,1)S(1)}, bf16[2,2,1024]{2,1,0:T(2,128)(2,1)S(1)}, u32[]{:S(2)}, u32[]{:S(2)}) %collective-permute-start.1) | collective-permute-done | bytes 8224 | tf_op jit(solution)/shard_map/ppermute | solution.py:501
  427.4 1.2 copy-done.1
  428.7 1.4 multiply_reduce_fusion
  431.5 5.0 fusion.18
  436.6 1.0 copy.105
  437.9 4.5 fusion.22
  442.4 10.2 %fusion.20 = f32[1024,3072]{1,0:T(8,128)} fusion(bf16[512,1024]{1,0:T(8,128)(2,1)} %copy-done.10, bf16[512,1024]{1,0:T(8,128)(2,1)} %copy-done.12, bf16[512,1024]{1,0:T(8,128)(2,1)} %copy-done.9, bf16[512,1024]{1,0:T(8,128)(2,1)} %copy-done.11), kind=kOutput, calls=%fused_computation.42 | convolution fusion | flops 3230662656 | bytes 16777216 | tf_op jit(solution)/shard_map/dot_general | solution.py:505
  452.6 1.1 slice_bitcast_fusion
  456.0 1.8 copy.101
  457.8 1.7 copy.96
  459.5 1.7 fusion.31
  461.2 1.8 reshape.147
  463.0 1.7 copy.131
  465.4 1.1 reshape.150
  467.3 1.1 reshape.148
  468.4 1.3 maximum_convert_fusion.2
  469.7 1.6 copy.97
  471.4 3.0 reshape.154
  474.4 0.9 reshape.151
  475.3 1.0 copy.128
  476.3 1.2 maximum_convert_fusion.3
  477.5 1.6 copy.102
  479.1 3.0 reshape.155
  482.1 3.1 fusion.17
  485.2 89.5 %reduce-scatter.10.cloned.1.call-done = f32[32,5]{1,0:T(8,128)} async-done(((f32[1024,5]{1,0:T(8,128)}), f32[32,5]{1,0:T(8,128)}) %reduce-scatter.10.cloned.1.call-update) | async-done | bytes 656
  576.2 0.9 fusion.33
  578.2 144.1 %reduce-scatter.8.cloned.1.call-done = f32[32,1024]{1,0:T(8,128)} async-done(((f32[1024,1024]{1,0:T(8,128)}), f32[32,1024]{1,0:T(8,128)}) %reduce-scatter.8.cloned.1.call-update) | async-done | bytes 131088 | tf_op jit(solution)/shard_map/reduce_scatter | solution.py:790
  722.3 161.8 %reduce-scatter.6.cloned.1.call-done = f32[32,3072]{1,0:T(8,128)} async-done(((f32[1024,3072]{1,0:T(8,128)}), f32[32,3072]{1,0:T(8,128)}) %reduce-scatter.6.cloned.1.call-update) | async-done | bytes 393232 | tf_op jit(solution)/shard_map/reduce_scatter | solution.py:789
  884.1 1.9 copy.134
  (122 shorter events, 17.0 us)
Async XLA Ops:
  7.2 5.7 copy-start.21
  7.2 5.7 copy-start.22
  7.2 76.9 %copy-start.16 = (f32[32,4608]{1,0:T(8,128)S(1)}, f32[32,4608]{1,0:T(8,128)}, u32[]{:S(2)}) copy-start(f32[32,4608]{1,0:T(8,128)} %param.18) | copy-start | bytes 1769476
  7.2 83.2 %all-gather.4.cloned.1.call-start = ((), (), s32[]{:S(2)}) async-start(), calls=%async_computation.3 | async-start | bytes 6488064 | tf_op jit(solution)/shard_map/all_gather | solution.py:731
  9.0 133.4 %all-gather.6.cloned.1.call-start = ((), (), s32[]{:S(2)}) async-start(), calls=%async_computation.4 | async-start | bytes 2162688 | tf_op jit(solution)/shard_map/all_gather | solution.py:732
  10.6 564.1 %reduce-scatter.10.cloned.1.call-start = ((), (), s32[]{:S(2)}) async-start(), calls=%async_computation.7 | async-start | bytes 540672
  84.1 1.5 copy-start.20
  85.0 1.6 copy-start.17
  88.3 1.8 copy-start.6
  90.4 5.9 copy-start.10
  96.3 4.3 copy-start.2
  96.3 1.8 copy-start.18
  96.7 2.8 collective-permute-start
  99.8 1.3 copy-start
  101.1 1.4 copy-start.3
  102.9 42.5 %copy-start.8 = (bf16[512,1024]{1,0:T(8,128)(2,1)}, bf16[512,1024]{1,0:T(8,128)(2,1)S(1)}, u32[]{:S(2)}) copy-start(bf16[512,1024]{1,0:T(8,128)(2,1)S(1)} %fusion.6) | copy-start | bytes 3145732
  145.4 1.4 copy-start.5
  393.2 7.9 slice-start
  396.2 5.0 slice-start.1
  396.2 5.0 copy-start.4
  396.2 5.1 copy-start.13
  402.6 28.4 %copy-start.9 = (bf16[512,1024]{1,0:T(8,128)(2,1)}, bf16[512,1024]{1,0:T(8,128)(2,1)S(1)}, u32[]{:S(2)}) copy-start(bf16[512,1024]{1,0:T(8,128)(2,1)S(1)} %get-tuple-element.78) | copy-start | bytes 3145732
  402.6 24.2 %collective-permute-start.1 = (bf16[2,2,1024]{2,1,0:T(2,128)(2,1)S(1)}, bf16[2,2,1024]{2,1,0:T(2,128)(2,1)S(1)}, u32[]{:S(2)}, u32[]{:S(2)}) collective-permute-start(bf16[2,2,1024]{2,1,0:T(2,128)(2,1)S(1)} %slice.195), channel_id=1, source_target_pairs={{1,0},{2,1},{3,2},{5,4},{6,5},{7,6},{9,8},{10,9},{11,10},{13,12},{... | collective-permute-start | bytes 24584 | tf_op jit(solution)/shard_map/ppermute | solution.py:501
  427.1 1.6 copy-start.1
  427.1 4.0 slice-start.2
  428.7 2.4 slice-start.3
  430.1 1.4 copy-start.7
  431.0 5.5 copy-start.11
  431.0 5.5 copy-start.12
  437.6 284.7 %reduce-scatter.8.cloned.1.call-start = ((), (), s32[]{:S(2)}) async-start(), calls=%async_computation.6 | async-start | bytes 4325376 | tf_op jit(solution)/shard_map/reduce_scatter | solution.py:790
  442.4 441.7 %reduce-scatter.6.cloned.1.call-start = ((), (), s32[]{:S(2)}) async-start(), calls=%async_computation.5 | async-start | bytes 12976128 | tf_op jit(solution)/shard_map/reduce_scatter | solution.py:789
  453.7 0.7 copy-start.14
  469.7 4.7 copy-start.19
  469.7 6.5 copy-start.15
Sparse Core Ops, SparseCore 0:
  11.5 71.8 all-gather.3
  86.9 55.5 all-gather.5
  437.7 136.9 reduce-scatter.9
  577.6 144.7 reduce-scatter.7
  729.8 154.2 reduce-scatter.5

commit v2 on v1

--- a/solution.py
+++ b/solution.py
@@ -14,6 +14,7 @@
 NT = (((1,), (1,)), ((), ()))
 TN = (((0,), (0,)), ((), ()))
 TP = 4
+LANES = 128
 
 
 def mm(left, right, dims):
@@ -53,13 +54,14 @@
     def __init__(self):
         self.pending = []
 
-    def send(self, src, dst, ssem, rsem, device, pred=True):
+    def send(self, src, dst, ssem, rsem, device, pred=True, group=None):
         def make():
             return pltpu.make_async_remote_copy(
                 src_ref=src, dst_ref=dst, send_sem=ssem, recv_sem=rsem,
                 device_id=device, device_id_type=MESH)
         when(pred, lambda: make().start())
-        self.pending.append((pred, make))
+        if group is None:
+            self.pending.append((pred, make))
 
     def local(self, src, dst, sem):
         pltpu.make_async_copy(src, dst, sem).start()
@@ -493,6 +495,300 @@
         compiler_params=pltpu.CompilerParams(
             collective_id=cid, has_side_effects=True, vmem_limit_bytes=66_900_000),
     )(h, df, gus, ds)
+
+
+def pieces_of(width):
+    half = width // 2
+    return (
+        (0, 0, width, "xzy"),
+        (1, 0, width, "yzx"),
+        (2, 0, width, "zxy"),
+        (3, 0, half, "xzy"),
+        (3, half, half, "yzx"),
+        (4, 0, LANES, "zxy"),
+    )
+
+
+def gather_sems(nz, count):
+    D = pltpu.SemaphoreType.DMA
+    return [D((count, 2, 2, nz)), D((count, 2, nz)), D((count, nz)), D((count, nz)), D((count, 2, nz)),
+            D((count, 2, nz)), D((count,)), D((count,))]
+
+
+def gather_flow(p, cp, n, piece, W, sems):
+    s_z, r_z, s_1, r_1, s_2, r_2, s_c, r_c = sems
+    _, c0, cn, order = piece
+    cs = slice(c0, c0 + cn)
+    z, nz = p.z, p.nz
+    inner_l, inner_r = z > 0, z < nz - 1
+    a_is_x = order != "yzx"
+
+    def blk(a, b, zz, c=None):
+        y, x = (b, a) if a_is_x else (a, b)
+        return W.at[y, x, p.c if c is None else c, zz, :, cs]
+    a, b = (p.x, p.y) if a_is_x else (p.y, p.x)
+
+    def other(axis):
+        return p.at(i=p.member(2)) if axis == "x" else p.at(y=1 - p.y)
+    axis_a, axis_b = ("x", "y") if a_is_x else ("y", "x")
+
+    def core(aa, bb, zz, pred=True):
+        r = blk(aa, bb, zz)
+        cp.send(r, r, s_c.at[n], r_c.at[n], p.at(i=p.member(1)), pred, group=(n, "c"))
+
+    def zsend(aa, zz, right, pred):
+        r = blk(aa, b, zz)
+        cp.send(r, r, s_z.at[n, aa, 1 if right else 0, zz], r_z.at[n, aa, zz],
+                p.at(z=z + 1 if right else z - 1), pred)
+
+    def asend(zz, pred=True):
+        r = blk(a, b, zz)
+        cp.send(r, r, s_1.at[n, zz], r_1.at[n, zz], other(axis_a), pred)
+
+    def bsend(aa, zz, pred=True):
+        r = blk(aa, b, zz)
+        cp.send(r, r, s_2.at[n, aa, zz], r_2.at[n, aa, zz], other(axis_b), pred)
+
+    zfirst = order == "zxy"
+    asend(z)
+    zsend(a, z, True, inner_r)
+    zsend(a, z, False, inner_l)
+    bsend(a, z)
+    core(a, b, z)
+    if not zfirst:
+        yield
+        cp.arrived(blk(1 - a, b, z), s_1.at[n, z], r_1.at[n, z], p.at())
+        zsend(1 - a, z, True, inner_r)
+        zsend(1 - a, z, False, inner_l)
+        bsend(1 - a, z)
+        core(1 - a, b, z)
+    for s in range(1, nz):
+        for right in (True, False):
+            yield
+            zz = z - s if right else z + s
+            got = zz >= 0 if right else zz <= nz - 1
+            more = got & (inner_r if right else inner_l)
+            for aa in ((a,) if zfirst else (a, 1 - a)):
+                pl.when(got)(lambda aa=aa, zz=zz: cp.arrived(
+                    blk(aa, b, zz), s_z.at[n, aa, 0, zz], r_z.at[n, aa, zz], p.at()))
+                zsend(aa, zz, right, more)
+                if zfirst:
+                    asend(zz, got)
+                bsend(aa, zz, got)
+                core(aa, b, zz, got)
+    if zfirst:
+        for zz in range(nz):
+            yield
+            cp.arrived(blk(1 - a, b, zz), s_1.at[n, zz], r_1.at[n, zz], p.at())
+            bsend(1 - a, zz)
+            core(1 - a, b, zz)
+    for zz in range(nz):
+        for aa in (a, 1 - a):
+            yield
+            cp.arrived(blk(aa, 1 - b, zz), s_2.at[n, aa, zz], r_2.at[n, aa, zz], p.at())
+            core(aa, 1 - b, zz)
+    yield
+    cp.arrived(W.at[:, :, 1 - p.c, :, :, cs], s_c.at[n], r_c.at[n], p.at())
+    cp.pending.append((True, lambda: pltpu.make_async_remote_copy(
+        src_ref=W.at[:, :, p.c, :, :, cs], dst_ref=W.at[:, :, p.c, :, :, cs], send_sem=s_c.at[n],
+        recv_sem=r_c.at[n], device_id=p.at(i=p.member(1)), device_id_type=MESH)))
+
+
+def sum_sems(nz, count):
+    D = pltpu.SemaphoreType.DMA
+    return [D((count,)), D((count,)), D((count, nz)), D((count, nz)), D((count, nz)), D((count, nz)),
+            D((count, 2, nz)), D((count, nz + 1))]
+
+
+def sum_scratch(nz, shard, pieces):
+    core = [pltpu.VMEM((2, 2, nz, shard, q[2]), BF) for q in pieces]
+    one = [pltpu.VMEM((2, nz, shard, q[2]), BF) for q in pieces]
+    two = [pltpu.VMEM((nz if q[3] == "zxy" else 1, shard, q[2]), BF) for q in pieces]
+    path = [pltpu.VMEM((nz + 1, 1 if q[3] == "zxy" else 2, shard, q[2]), BF) for q in pieces]
+    return [core, one, two, path]
+
+
+def sum_flow(p, cp, n, piece, G, land, out, sems):
+    s_c, r_c, s_1, r_1, s_2, r_2, s_z, r_z = sems
+    LC, L1, L2, LZ = (l[n] for l in land)
+    _, c0, cn, order = piece
+    cs = slice(c0, c0 + cn)
+    z, nz = p.z, p.nz
+    inner_l, inner_r = z > 0, z < nz - 1
+    targets = [nz - 1, 0] + list(range(1, nz - 1))[::-1]
+    zlast = order == "zxy"
+    b_is_y = order != "yzx"
+    b, a = (p.y, p.x) if b_is_y else (p.x, p.y)
+    dev_b = p.at(y=1 - p.y) if b_is_y else p.at(i=p.member(2))
+    dev_a = p.at(i=p.member(2)) if b_is_y else p.at(y=1 - p.y)
+
+    def g(bb, aa, zz):
+        y, x = (bb, aa) if b_is_y else (aa, bb)
+        return (y, x, p.c, zz, slice(None), cs)
+
+    def f(v):
+        return v.astype(F32)
+
+    cp.send(G.at[:, :, 1 - p.c, :, :, cs], LC, s_c.at[n], r_c.at[n], p.at(i=p.member(1)))
+    pl.when(jnp.logical_not(inner_l))(lambda: LZ.__setitem__(0, jnp.zeros(LZ.shape[1:], BF)))
+    pl.when(jnp.logical_not(inner_r))(lambda: LZ.__setitem__(nz, jnp.zeros(LZ.shape[1:], BF)))
+    yield
+    cp.arrived(LC, s_c.at[n], r_c.at[n], p.at())
+
+    def lc(bb, aa, zz):
+        y, x = (bb, aa) if b_is_y else (aa, bb)
+        return (y, x, zz)
+    for zz in targets:
+        for aa in range(2):
+            i = g(1 - b, aa, zz)
+            G[i] = (f(G[i]) + f(LC[lc(1 - b, aa, zz)])).astype(BF)
+        y, x = (1 - b, slice(None)) if b_is_y else (slice(None), 1 - b)
+        cp.send(G.at[y, x, p.c, zz, :, cs], L1.at[:, zz], s_1.at[n, zz], r_1.at[n, zz], dev_b)
+    for zz in targets:
+        for aa in range(2):
+            i = g(b, aa, zz)
+            G[i] = (f(G[i]) + f(LC[lc(b, aa, zz)])).astype(BF)
+    if zlast:
+        for zz in targets:
+            yield
+            cp.arrived(L1.at[:, zz], s_1.at[n, zz], r_1.at[n, zz], p.at())
+            i = g(b, 1 - a, zz)
+            G[i] = (f(G[i]) + f(L1[1 - a, zz])).astype(BF)
+            cp.send(G.at[i], L2.at[zz], s_2.at[n, zz], r_2.at[n, zz], dev_a)
+
+    def own(zz, k):
+        if zlast:
+            return f(G[g(b, a, zz)]) + f(L1[a, zz]) + f(L2[zz])
+        return f(G[g(b, k, zz)]) + f(L1[k, zz])
+
+    def put(zz, k, v):
+        G[g(b, a if zlast else k, zz)] = v.astype(BF)
+    ks = range(1) if zlast else range(2)
+
+    def zwait(sl):
+        cp.arrived(LZ.at[sl], s_z.at[n, 0, 0], r_z.at[n, sl], p.at())
+    for zz in targets:
+        yield
+        if zlast:
+            cp.arrived(L2.at[zz], s_2.at[n, zz], r_2.at[n, zz], p.at())
+        else:
+            cp.arrived(L1.at[:, zz], s_1.at[n, zz], r_1.at[n, zz], p.at())
+        right, left = z < zz, z > zz
+        both = (right & inner_l) | (left & inner_r)
+
+        def add3(zz=zz):
+            zwait(zz)
+            for k in ks:
+                put(zz, k, own(zz, k) + f(LZ[zz, k]))
+
+        def add2(zz=zz):
+            for k in ks:
+                put(zz, k, own(zz, k))
+        pl.when(both)(add3)
+        pl.when(jnp.logical_and(z != zz, jnp.logical_not(both)))(add2)
+        if zlast:
+            src = G.at[p.y, pl.ds(p.x, 1), p.c, zz, :, cs]
+        elif b_is_y:
+            src = G.at[p.y, :, p.c, zz, :, cs]
+        else:
+            src = G.at[:, p.x, p.c, zz, :, cs]
+        cp.send(src, LZ.at[zz], s_z.at[n, 1, zz], r_z.at[n, zz], p.at(z=z + 1), right)
+        sl = jnp.where(z - 1 == zz, nz, zz)
+        cp.send(src, LZ.at[sl], s_z.at[n, 0, zz], r_z.at[n, sl], p.at(z=z - 1), left)
+    yield
+    pl.when(inner_l)(lambda: zwait(z))
+    pl.when(inner_r)(lambda: zwait(nz))
+
+    def total(k):
+        return own(z, k) + f(LZ[z, k]) + f(LZ[nz, k])
+    if zlast:
+        out[:, cs] = total(0)
+        return
+    G[g(b, 1 - a, z)] = total(1 - a).astype(BF)
+    cp.send(G.at[g(b, 1 - a, z)], L2.at[0], s_2.at[n, 0], r_2.at[n, 0], dev_a)
+    out[:, cs] = total(a)
+    yield
+    cp.arrived(L2.at[0], s_2.at[n, 0], r_2.at[n, 0], p.at())
+    out[:, cs] += f(L2[0])
+
+
+def interleave(flows):
+    flows = list(flows)
+    while flows:
+        for flow in list(flows):
+            if next(flow, "end") == "end":
+                flows.remove(flow)
+
+
+def gather_body(nz, pieces, *refs):
+    blocks, outs = refs[:5], refs[5:10]
+    sem_l, sems = refs[10], refs[11:]
+    p, cp = Place(nz), Copies()
+    for q in range(5):
+        cp.local(blocks[q], outs[q].at[p.y, p.x, p.c, p.z], sem_l.at[q])
+    entry_barrier(p)
+    for q in range(5):
+        pltpu.make_async_copy(blocks[q], outs[q].at[p.y, p.x, p.c, p.z], sem_l.at[q]).wait()
+    interleave(gather_flow(p, cp, n, piece, outs[piece[0]], sems) for n, piece in enumerate(pieces))
+    cp.drain()
+
+
+def gather_call(blocks, nz, cid):
+    shard, width = blocks[0].shape
+    pieces = pieces_of(width)
+    A = pl.BlockSpec(memory_space=pl.ANY)
+    V = pl.BlockSpec(memory_space=pltpu.VMEM)
+    outs = [jax.ShapeDtypeStruct((2, 2, 2, nz, shard, b.shape[1]), BF) for b in blocks]
+    return pl.pallas_call(
+        functools.partial(gather_body, nz, pieces),
+        name="mixer_gather",
+        out_shape=outs,
+        in_specs=[V] * 5,
+        out_specs=[A] * 5,
+        scratch_shapes=[pltpu.SemaphoreType.DMA((5,))] + gather_sems(nz, len(pieces)),
+        compiler_params=pltpu.CompilerParams(collective_id=cid, has_side_effects=True),
+    )(*blocks)
+
+
+def sum_body(nz, pieces, *refs):
+    g_in, g_out, g_small = refs[:3]
+    outs = refs[3:8]
+    G = refs[8:13]
+    land = refs[13:17]
+    sem_l, sems = refs[17], refs[18:]
+    p, cp = Place(nz), Copies()
+    width = g_out.shape[-1]
+
+    def pairs():
+        return [(g_in.at[:, :, :, :, :, q * width:(q + 1) * width], G[q]) for q in range(3)] + [
+            (g_out, G[3]), (g_small, G[4])]
+    for q, (src, dst) in enumerate(pairs()):
+        cp.local(src, dst, sem_l.at[q])
+    entry_barrier(p)
+    for q, (src, dst) in enumerate(pairs()):
+        pltpu.make_async_copy(src, dst, sem_l.at[q]).wait()
+    interleave(sum_flow(p, cp, n, piece, G[piece[0]], land, outs[piece[0]], sems) for n, piece in enumerate(pieces))
+    cp.drain()
+
+
+def sum_call(g_in, g_out, g_small, nz, cid):
+    width = g_out.shape[-1]
+    shard = g_out.shape[0] // (8 * nz)
+    pieces = pieces_of(width)
+    A = pl.BlockSpec(memory_space=pl.ANY)
+    V = pl.BlockSpec(memory_space=pltpu.VMEM)
+    view = lambda v: v.reshape(2, 2, 2, nz, shard, v.shape[-1])
+    wide = [width] * 4 + [LANES]
+    return pl.pallas_call(
+        functools.partial(sum_body, nz, pieces),
+        name="mixer_sum",
+        out_shape=[jax.ShapeDtypeStruct((shard, w), F32) for w in wide],
+        in_specs=[A] * 3,
+        out_specs=[V] * 5,
+        scratch_shapes=[pltpu.VMEM((2, 2, 2, nz, shard, w), BF) for w in wide] + sum_scratch(nz, shard, pieces)
+        + [pltpu.SemaphoreType.DMA((5,))] + sum_sems(nz, len(pieces)),
+        compiler_params=pltpu.CompilerParams(collective_id=cid, has_side_effects=True, vmem_limit_bytes=66_900_000),
+    )(view(g_in), view(g_out), view(g_small))
 
 
 def shifted(block, axis, distance):
@@ -726,12 +1022,15 @@
     nz = lax.axis_size("seq")
     ny = lax.axis_size("dp") // TP
     rows = micro * count
-    both = ("dp", "seq")
     x = tokens.reshape(rows, width).astype(F32)
-    w_in = lax.all_gather(in_weight.astype(BF), both, axis=0, tiled=True)
-    w_out = lax.all_gather(out_weight.astype(BF), both, axis=0, tiled=True)
+    low_in = in_weight.astype(BF)
     small = jnp.concatenate([ln1_gain[None], ln2_gain[None], conv_kernel], axis=0).astype(BF)
-    small = lax.all_gather(small, both, axis=1, tiled=True).astype(F32)
+    small = jnp.pad(small.T, ((0, 0), (0, LANES - taps - 2)))
+    blocks = [low_in[:, q * width : (q + 1) * width] for q in range(3)]
+    blocks += [out_weight.astype(BF), small]
+    gathered = gather_call(blocks, nz, 1)
+    w_b, w_c, w_u, w_out, small = (v.reshape(width, -1) for v in gathered)
+    small = small[:, : taps + 2].T.astype(F32)
     gain_one, gain_two, kernel = small[0], small[1], small[2:]
 
     offset = lax.axis_index("seq") * count
@@ -744,8 +1043,7 @@
     ]
     inv1, norm1 = norm_parts(x)
     h1 = (norm1 * gain_one).astype(BF)
-    proj = matmul(h1, w_in)
-    b, c, u = (proj[:, k * width : (k + 1) * width] for k in range(3))
+    b, c, u = (matmul(h1, w) for w in (w_b, w_c, w_u))
     mixed = (b * u).astype(BF).reshape(micro, count, width)
     prev = shifted(mixed[:, count - 2 :], "seq", 1)
     ext = jnp.concatenate([prev, mixed], axis=1).astype(F32)
@@ -767,7 +1065,7 @@
     dr = df.astype(F32) + norm_back(dh2, norm2, inv2, gain_two)
     do = dr.astype(BF)
     dy = matmul(do, w_out.T)
-    g_out = matmul(gated.T, do)
+    g_out = matmul(gated.T, do).astype(BF)
     dc = dy * conv
     dconv = (dy * c).astype(BF).reshape(micro, count, width)
     after = shifted(dconv[:, :2], "seq", -1)
@@ -779,15 +1077,17 @@
         dmix = dmix + kernel[t] * weighted[:, 2 - t : 2 - t + count]
         kterms.append(jnp.sum(weighted[:, :count] * ext[:, t : t + count], axis=(0, 1)))
     dmix = dmix.reshape(rows, width)
-    dproj = jnp.concatenate([dmix * u, dc, dmix * b], axis=1).astype(BF)
-    dh1 = matmul(dproj, w_in.T)
-    g_in = matmul(h1.T, dproj)
+    dps = [v.astype(BF) for v in (dmix * u, dc, dmix * b)]
+    dh1 = sum(matmul(v, w.T) for v, w in zip(dps, (w_b, w_c, w_u)))
+    g_in = matmul(h1.T, jnp.concatenate(dps, axis=1)).astype(BF)
     g_gain1 = jnp.sum(dh1 * norm1, axis=0)
     gx = (dr + norm_back(dh1, norm1, inv1, gain_one)).astype(BF)
     g_small = jnp.stack([g_gain1, g_gain2] + kterms, axis=0)
-    g_small = lax.psum_scatter(g_small, both, scatter_dimension=1, tiled=True)
-    g_in = lax.psum_scatter(g_in, both, scatter_dimension=0, tiled=True)
-    g_out = lax.psum_scatter(g_out, both, scatter_dimension=0, tiled=True)
+    g_small = jnp.pad(g_small.T, ((0, 0), (0, LANES - taps - 2))).astype(BF)
+    sums = sum_call(g_in, g_out, g_small, nz, 2)
+    g_in = jnp.concatenate(sums[:3], axis=1)
+    g_out = sums[3]
+    g_small = sums[4][:, : taps + 2].T
     shape = tokens.shape
     return (
         output.reshape(shape), gx.reshape(shape), g_small[0], g_in, g_small[2:], g_out,

time: 901 us -> 512 us (0.57)
  waiting for transfers between devices: 458 us -> 9.53 us
  Pallas kernels: 245 us -> 392 us
  blocking collectives: 71.1 us -> 0 us
  between operations: 14.9 us -> 1.45 us
    reduce_scatter x2 -> x0, waiting for transfers between devices: 306 us -> none  [the longest x1 162 us: fast_device(): g_in = lax.psum_scatter(g_in, both, scatter_dimension=0, tiled=True)]
    pallas_call x0 -> x2, Pallas kernels: none -> 144 us  [the longest x1 94.8 us: sum_call(): pl.pallas_call(functools.partial(sum_body, nz, pieces), name='mixer_sum',...]
    unnamed x6 -> x0, waiting for transfers between devices: 89.6 us -> none
    all_gather x1 -> x0, blocking collectives: 71.1 us -> none  [fast_device(): small = lax.all_gather(small, both, axis=1, tiled=True).astype(F32)]
    all_gather x2 -> x0, waiting for transfers between devices: 39.5 us -> none  [the longest x1 39.5 us: fast_device(): w_out = lax.all_gather(out_weight.astype(BF), both, axis=0, tiled=True)]
    ppermute x2, waiting for transfers between devices: 23.2 us -> 9.53 us  [shifted(): return lax.ppermute(block, axis, route)]
    reshape x10, local copies, waits for them, and re-layouts: 11.9 us -> 1.26 us  [join_columns(): g[:, :, npos * start:npos * (start + size)].reshape(TP, rows, ny, nz, size)]
    dot_general x6 -> x10, matrix products: 29.8 us -> 24.7 us  [matmul(): return jnp.dot(left, right, preferred_element_type=jnp.float32)]
  transfers between devices with their start and end apart: 7 -> 2, of which waited for: 6 -> 1; matrix products, arithmetic and copies ran while one was open for 8% -> 7% of each run, Pallas kernels for 0% -> 0%
where the time goes in v2:
time: 512 us; the launch traced here: 506 us
  Pallas kernels  392 us (77%)
  local copies, waits for them, and re-layouts  46.8 us (9%)
  other arithmetic  28.1 us (5%)
  matrix products  24.7 us (5%)
  waiting for transfers between devices  9.53 us (2%)
    pallas_call x1, Pallas kernels, ffn_call(): pl.pallas_call(functools.partial(ffn_body, parts, nz), name='ffn', out_sh...  248 us
    pallas_call x1, Pallas kernels, sum_call(): pl.pallas_call(functools.partial(sum_body, nz, pieces), name='mixer_sum',...  94.8 us
    pallas_call x1, Pallas kernels, gather_call(): pl.pallas_call(functools.partial(gather_body, nz, pieces), name='mixer_ga...  49.3 us
    dot_general x10, matrix products, matmul(): return jnp.dot(left, right, preferred_element_type=jnp.float32)  24.7 us
    unnamed x85, local copies, waits for them, and re-layouts  14 us
  transfers between devices with their start and end apart: 2, of which 1 were waited for; matrix products, arithmetic and copies ran while one was open for 7% of the time, Pallas kernels for 0%

profile of v2, /device:TPU:0, one launch (start us, length us, event | category | flops | bytes accessed | tf_op | source)
XLA Modules:
  0.0 505.9 jit_solution(3396650612765169434)
XLA Ops:
  0.7 1.1 convert_element_type.118
  2.4 1.5 convert_element_type.119.refs_3_
  6.1 49.3 %mixer_gather.1 = (bf16[2,2,2,4,32,1024]{5,4,3,2,1,0:T(8,128)(2,1)}, bf16[2,2,2,4,32,1024]{5,4,3,2,1,0:T(8,128)(2,1)}, bf16[2,2,2,4,32,1024]{5,4,3,2,1,0:T(8,128...) custom-call(bf16[32,1024]{1,0:T(8,128)(2,1)} %get-tuple-element.119.refs_0_, ...), custom_call_target="tpu_custom_call" | custom-call | tf_op jit(solution)/shard_map/mixer_gather/pallas_call | solution.py:742
  55.3 1.1 copy.124
  58.2 1.3 fusion.38
  59.8 2.7 multiply_convert_fusion.2
  63.1 2.0 collective-permute-start
  65.2 1.7 reshape.207
  66.9 2.1 fusion.33
  68.9 1.8 convert_element_type.130
  70.7 2.6 reshape.203
  73.4 2.0 fusion.32
  77.0 2.0 copy_bitcast_fusion
  79.0 1.8 reshape.209
  80.9 1.8 reshape.208
  83.7 1.9 copy_bitcast_fusion.2
  85.6 1.2 reshape.205
  86.8 0.9 reshape.204
  88.5 1.1 maximum_bitcast_fusion.1
  89.6 1.0 maximum_bitcast_fusion
  90.5 0.9 pad_maximum_fusion.gus
  92.3 1.0 maximum_convert_fusion
  94.7 1.1 copy-done.23
  95.7 2.6 fusion.11
  98.3 1.4 multiply_reduce_fusion.3
  99.7 1.3 copy-done.5
  101.0 1.2 multiply_convert_fusion.1.h_in
  102.2 247.8 %ffn.1 = (f32[512,1024]{1,0:T(8,128)}, f32[512,1024]{1,0:T(8,128)}, bf16[4,2,32,1152]{3,2,1,0:T(8,128)(2,1)}, f32[144,1024]{1,0:T(8,128)}) custom-call(bf16[512,1024]{1,0:T(8,128)(2,1)} %multiply_convert_fusion.1.h_in, bf16[512,1024]{1,0:T(8,128)(2,1)} %bitcast.150, bf16[4,2,32,1152]{3,2,1,0:T(8,128)(2,1)} %pad_maximum_fusion.gus, ...), custom_call_target="tpu_custom_call" | custom-call | tf_op jit(solution)/shard_map/ffn/pallas_call | solution.py:483
  350.0 1.3 slice_bitcast_fusion
  351.8 2.4 multiply_reduce_fusion.1
  354.3 3.5 multiply_add_fusion
  357.8 2.7 convolution_convert_fusion.1
  360.5 1.1 copy-done.9
  362.1 1.3 fusion.12
  363.5 1.3 collective-permute-start.1
  364.8 2.7 fusion.40
  370.3 1.8 reshape.225
  372.8 1.8 reshape.226
  374.5 9.5 %collective-permute-done.1 = bf16[2,2,1024]{2,1,0:T(2,128)(2,1)S(1)} collective-permute-done((bf16[2,2,1024]{2,1,0:T(2,128)(2,1)S(1)}, bf16[2,2,1024]{2,1,0:T(2,128)(2,1)S(1)}, u32[]{:S(2)}, u32[]{:S(2)}) %collective-permute-start.1) | collective-permute-done | bytes 8224 | tf_op jit(solution)/shard_map/ppermute | solution.py:797
  384.7 1.2 copy-done.1
  385.9 1.6 multiply_reduce_fusion
  388.1 0.8 fusion.10
  389.7 1.3 fusion.39
  392.3 3.1 fusion.23
  395.4 5.8 %convolution_convert_fusion = bf16[1024,3072]{1,0:T(8,128)(2,1)} fusion(bf16[512,1024]{1,0:T(8,128)(2,1)S(1)} %get-tuple-element.106, bf16[512,1024]{1,0:T(8,128)(2,1)S(1)} %get-tuple-element.98, bf16[512,1024]{1,0:T(8,128)(2,1)S(1)} %copy-done.27, bf16[512,1024]{1,0:T(8,128)(2,1)S(1)} %get-tuple-element.99), kind=kOutput, calls=%fused_computation | convolution fusion | flops 3233808384 | bytes 10485760 | tf_op jit(solution)/shard_map/dot_general | solution.py:801
  402.2 94.8 %mixer_sum.1 = (f32[32,1024]{1,0:T(8,128)}, f32[32,1024]{1,0:T(8,128)}, f32[32,1024]{1,0:T(8,128)}, f32[32,1024]{1,0:T(8,128)}, f32[32,128]{1,0:T(8,128)}) custom-call(bf16[2,2,2,4,32,3072]{5,4,3,2,1,0:T(8,128)(2,1)} %bitcast.149, bf16[2,2,2,4,32,1024]{5,4,3,2,1,0:T(8,128)(2,1)} %bitcast.159, bf16[2,2,2,4,32,128]{5,4,3,2,1,0:T(8,128)(2,1)} %bitcast.161), custom_call_target="tpu_custom_call" | custom-call | tf_op jit(solution)/shard_map/mixer_sum/pallas_call | solution.py:782
  499.2 4.2 fusion.21
  504.8 0.8 copy.150
  (142 shorter events, 23.7 us)
Async XLA Ops:
  0.6 56.4 %copy-start.7 = (bf16[2,1,256,1024]{3,2,1,0:T(8,128)(2,1)S(1)}, bf16[2,1,256,1024]{3,2,1,0:T(8,128)(2,1)}, u32[]{:S(2)}) copy-start(bf16[2,1,256,1024]{3,2,1,0:T(8,128)(2,1)} %param.11) | copy-start | bytes 3145732
  56.4 1.8 copy-start.19
  58.2 1.6 copy-start.21
  59.5 3.0 copy-start.10
  59.8 5.3 %copy-start.28 = (f32[32,4608]{1,0:T(8,128)S(1)}, f32[32,4608]{1,0:T(8,128)}, u32[]{:S(2)}) copy-start(f32[32,4608]{1,0:T(8,128)} %param.19) | copy-start | bytes 1769476
  63.1 29.1 %collective-permute-start = (bf16[2,2,1024]{2,1,0:T(2,128)(2,1)}, bf16[2,2,1024]{2,1,0:T(2,128)(2,1)}, u32[]{:S(2)}, u32[]{:S(2)}) collective-permute-start(bf16[2,2,1024]{2,1,0:T(2,128)(2,1)} %slice.189), channel_id=1, source_target_pairs={{0,1},{1,2},{2,3},{4,5},{5,6},{6,7},{8,9},{9,10},{10,11},{12,13},{... | collective-permute-start | bytes 24584 | tf_op jit(solution)/shard_map/ppermute | solution.py:797
  66.9 8.5 %copy-start.37 = (s32[2,1,1024]{2,1,0:T(1,128)S(1)}, s32[2,1,1024]{2,1,0:T(1,128)}, u32[]{:S(2)}) copy-start(s32[2,1,1024]{2,1,0:T(1,128)} %param.12) | copy-start | bytes 24580
  66.9 9.1 %slice-start = ((bf16[32,2,4,4,144]{4,3,2,1,0:T(4,128)(2,1)}), bf16[32,2,4,4,16]{4,3,2,1,0:T(4,128)(2,1)S(1)}, s32[]{:S(2)}) async-start(bf16[32,2,4,4,144]{4,3,2,1,0:T(4,128)(2,1)} %reshape.207), calls=%async_computation | async-start | bytes 524288 | tf_op jit(solution)/shard_map/slice | solution.py:990
  76.3 6.4 %slice-start.1 = ((bf16[32,2,4,4,144]{4,3,2,1,0:T(4,128)(2,1)}), bf16[32,2,4,4,16]{4,3,2,1,0:T(4,128)(2,1)S(1)}, s32[]{:S(2)}) async-start(bf16[32,2,4,4,144]{4,3,2,1,0:T(4,128)(2,1)} %reshape.203), calls=%async_computation.1 | async-start | bytes 524288 | tf_op jit(solution)/shard_map/slice | solution.py:990
  87.7 4.6 copy-start.36
  88.5 3.0 copy-start.29
  91.4 1.9 copy-start.35
  93.3 1.4 copy-start
  93.3 2.4 copy-start.23
  94.7 3.7 copy-start.2
  95.7 2.6 copy-start.17
  98.3 1.4 copy-start.15
  99.7 1.3 copy-start.5
  350.0 1.8 copy-start.6
  351.8 2.4 copy-start.13
  351.8 2.5 copy-start.14
  354.3 3.5 copy-start.16
  357.8 2.7 copy-start.4
  357.8 2.7 copy-start.3
  357.8 3.7 copy-start.9
  357.8 4.4 copy-start.18
  362.1 2.7 copy-start.24
  363.5 1.3 copy-start.26
  363.5 20.5 %collective-permute-start.1 = (bf16[2,2,1024]{2,1,0:T(2,128)(2,1)S(1)}, bf16[2,2,1024]{2,1,0:T(2,128)(2,1)S(1)}, u32[]{:S(2)}, u32[]{:S(2)}) collective-permute-start(bf16[2,2,1024]{2,1,0:T(2,128)(2,1)S(1)} %slice.204), channel_id=1, source_target_pairs={{1,0},{2,1},{3,2},{5,4},{6,5},{7,6},{9,8},{10,9},{11,10},{13,12},{... | collective-permute-start | bytes 24584 | tf_op jit(solution)/shard_map/ppermute | solution.py:797
  384.3 1.6 copy-start.1
  385.9 1.6 copy-start.11
  385.9 2.2 copy-start.12
  388.1 1.6 copy-start.22
  389.7 1.3 copy-start.8
  389.7 1.9 copy-start.20
  389.7 2.5 copy-start.25
  392.3 3.1 copy-start.27
  499.2 4.2 copy-start.32
  499.2 4.2 copy-start.33
  499.2 4.2 copy-start.34
  499.2 5.0 copy-start.31
  499.2 5.6 %copy-start.30 = (f32[144,1024]{1,0:T(8,128)S(1)}, f32[144,1024]{1,0:T(8,128)}, u32[]{:S(2)}) copy-start(f32[144,1024]{1,0:T(8,128)} %get-tuple-element.163) | copy-start | bytes 1769476
